TPU v7x, 256 devices: a whole 4x4x8 slice. The times are simulated.
256 devices in a mesh: seq: 64 (over x, y, z_hi, core), tp: 4 (over z_lo).
Axes of the slice: x: 4, y: 4, z: 8 (z_hi: 2, z_lo: 4; z = z_hi * 4 + z_lo), core: 2. Of those that a mesh axis runs over, the one named last changes fastest.
Arguments:
- hidden: bfloat16 [64, 512, 2048], P('seq', 'tp'), may hold values from -6 to 6
- norm_gain: bfloat16 [2048], replicated, may hold values from 0.099609375 to 1.8984375
- qkv_weight: bfloat16 [2048, 3, 2048], P(None, None, 'tp'), may hold values from -0.0625 to 0.0625
- out_weight: bfloat16 [2048, 2048], P('tp'), may hold values from -0.25 to 0.25
- bias_table: float32 [32, 32], P(None, 'tp'), may hold values from -4 to 4
- prefix_cache: bfloat16 [512, 2, 2048], P('seq', None, 'tp'), may hold values from -64 to 64
- suffix_lengths: int32 [64], replicated, may hold values from 64 to 512, as said below
- request_of_slot: int32 [64], replicated, may hold values from 0 to 63, each once
- block_of_slot: int32 [64], replicated, may hold values from 0 to 63, each once
- bias_bucket: int32 [640], replicated, may hold values from 0 to 31
Outputs:
- attended: bfloat16 [64, 512, 2048], P('seq', 'tp')
Inputs may be any that keep to these rules, and one draw needn't show every extreme that they name: `suffix_lengths`: every suffix holds 64 to 512 tokens, and some request holds exactly 512.
All inputs are finite; a program needn't handle non-finite values.
Results may differ from a plain program's by a relative error of at most 0.012.
The roundings to bfloat16 on the way count: a program that leaves them out, or rounds other values in their place, can miss the bound.
Values may be sent and summed in bfloat16 or wider, within the bound.
A program may use at most 320 MiB of HBM per device.

v0:
```python
import jax
import jax.numpy as jnp
from jax import lax
from jax.sharding import PartitionSpec as P

G = 4


def body(
    hidden,
    norm_gain,
    qkv_weight,
    out_weight,
    bias_table,
    prefix_cache,
    suffix_lengths,
    request_of_slot,
    block_of_slot,
    bias_bucket,
):
    seq_count = lax.axis_size("seq")
    tp_count = lax.axis_size("tp")
    rows_local = hidden.shape[1]
    slot_len = rows_local * tp_count
    width = hidden.shape[2]
    local_heads = bias_table.shape[1]
    local_cols = qkv_weight.shape[2]
    head_size = local_cols // local_heads
    block_rows = prefix_cache.shape[0]
    group_blocks = seq_count // G
    prefix_len = block_rows * group_blocks
    total_requests = suffix_lengths.shape[0]
    dist_count = bias_bucket.shape[0]
    bucket_count = bias_table.shape[0]
    request = lax.dynamic_index_in_dim(request_of_slot, lax.axis_index("seq"), 0, keepdims=False)
    group = request // (total_requests // G)
    length = lax.dynamic_index_in_dim(suffix_lengths, request, 0, keepdims=False)
    gain_f = norm_gain.astype(jnp.float32)
    weights = qkv_weight.reshape(width, 3 * local_cols)
    states = lax.all_gather(hidden, "tp", axis=1, tiled=True).reshape(-1, width).astype(jnp.float32)
    normed = (
        states * lax.rsqrt(jnp.mean(states * states, -1, keepdims=True) + 1e-06) * gain_f
    ).astype(jnp.bfloat16)
    qkv = jnp.dot(normed, weights, preferred_element_type=jnp.float32).astype(jnp.bfloat16)
    query_t = qkv[:, :local_cols].reshape(slot_len, local_heads, head_size).transpose(1, 2, 0)
    own_keys = (
        qkv[:, local_cols : 2 * local_cols]
        .reshape(slot_len, local_heads, head_size)
        .transpose(1, 0, 2)
    )
    own_values = (
        qkv[:, 2 * local_cols :].reshape(slot_len, local_heads, head_size).transpose(1, 0, 2)
    )
    one_hot = (bias_bucket[:, None] == jnp.arange(bucket_count)[None, :]).astype(jnp.float32)
    bias_t = jnp.dot(one_hot, bias_table, precision=lax.Precision.HIGHEST).T
    block_q = min(512, slot_len)
    query_blocks = slot_len // block_q

    def attend(state, key_rows, value_rows, key_pos, key_ok, first_query):
        running, denom, numer = state
        scores = jnp.einsum("hkd,hdq->hkq", key_rows, query_t, preferred_element_type=jnp.float32)
        query_pos = prefix_len + first_query + jnp.arange(block_q, dtype=jnp.int32)
        distance = query_pos[None, :] - key_pos[:, None]
        allowed = key_ok[:, None] & (distance >= 0)
        scores = scores + jnp.take(bias_t, jnp.clip(distance, 0, dist_count - 1), axis=1)
        scores = jnp.where(allowed[None], scores, -jnp.inf)
        updated = jnp.maximum(running, jnp.max(scores, 1))
        factor = jnp.exp(running - updated)
        probs = jnp.exp(scores - updated[:, None, :])
        denom = denom * factor + jnp.sum(probs, 1)
        numer = numer * factor[:, None, :] + jnp.einsum(
            "hkq,hkd->hdq",
            probs.astype(jnp.bfloat16),
            value_rows,
            preferred_element_type=jnp.float32,
        )
        return (updated, denom, numer)

    def all_queries(current, key_rows, value_rows, key_pos, key_ok):
        return tuple(
            (
                attend(current[qblock], key_rows, value_rows, key_pos, key_ok, qblock * block_q)
                for qblock in range(query_blocks)
            )
        )

    initial = tuple(
        (
            (
                jnp.full((local_heads, block_q), -1e30, jnp.float32),
                jnp.zeros((local_heads, block_q), jnp.float32),
                jnp.zeros((local_heads, head_size, block_q), jnp.float32),
            )
            for qblock in range(query_blocks)
        )
    )
    gathered = lax.all_gather(prefix_cache, "seq", axis=0, tiled=True)
    wanted = group * group_blocks + jnp.arange(group_blocks, dtype=jnp.int32)
    match = block_of_slot[None, :] == wanted[:, None]
    slot_ids = jnp.sum(jnp.where(match, jnp.arange(seq_count, dtype=jnp.int32)[None, :], 0), 1)
    picked = jnp.take(
        gathered.reshape(seq_count, block_rows, 2, local_cols), slot_ids, axis=0
    ).reshape(prefix_len, 2, local_cols)
    key_pos = jnp.arange(prefix_len, dtype=jnp.int32)
    key_ok = jnp.ones((prefix_len,), bool)
    key_block = min(512, prefix_len)
    count = picked.shape[0] // key_block
    packed = picked.reshape(count, key_block, 2, local_cols)
    pos_blocks = key_pos.reshape(count, key_block)
    ok_blocks = key_ok.reshape(count, key_block)

    def step(current, items):
        rows_block, pos_block, ok_block = items
        key_rows = rows_block[:, 0, :].reshape(key_block, local_heads, head_size).transpose(1, 0, 2)
        value_rows = (
            rows_block[:, 1, :].reshape(key_block, local_heads, head_size).transpose(1, 0, 2)
        )

        def compute(inner):
            return all_queries(inner, key_rows, value_rows, pos_block, ok_block)

        def keep_state(inner):
            return inner

        return (lax.cond(jnp.any(ok_block), compute, keep_state, current), None)

    result = list(lax.scan(step, initial, (packed, pos_blocks, ok_blocks))[0])
    qblock = 0
    key_pos = prefix_len + jnp.arange(block_q, dtype=jnp.int32)
    key_ok = jnp.ones((block_q,), bool)
    key_rows = own_keys
    value_rows = own_values
    result[qblock] = attend(result[qblock], key_rows, value_rows, key_pos, key_ok, qblock * block_q)
    final = tuple(result)
    outputs = jnp.concatenate([state[2] / state[1][:, None, :] for state in final], 2)
    attn = outputs.transpose(2, 0, 1).reshape(slot_len, local_cols).astype(jnp.bfloat16)
    product = jnp.dot(attn, out_weight, preferred_element_type=jnp.float32)
    alive = jnp.arange(rows_local * lax.axis_size("tp"), dtype=jnp.int32) < length
    summed = lax.psum_scatter(
        jnp.where(alive[:, None], product, 0.0).astype(jnp.bfloat16),
        "tp",
        scatter_dimension=0,
        tiled=True,
    )
    return summed[None]


def solution(mesh):
    return jax.shard_map(
        body,
        mesh=mesh,
        in_specs=(
            P("seq", "tp", None),
            P(),
            P(None, None, "tp"),
            P("tp", None),
            P(None, "tp"),
            P("seq", None, "tp"),
            P(),
            P(),
            P(),
            P(),
        ),
        out_specs=P("seq", "tp", None),
        check_vma=False,
    )
```

profile of v0, /device:TPU:1, one launch (start us, length us, event | category | flops | bytes accessed | tf_op | source)
XLA Modules:
  0.0 1291.4 jit_solution(1614467045178103539)
XLA Ops:
  6.5 0.0 copy-start
  6.5 0.0 all-gather.3.cloned.1.call-start
  6.5 1.5 copy.53
  8.0 0.0 all-gather.3.cloned.1.call-update
  8.0 0.0 all-gather.5.cloned.1.call-start
  8.1 0.7 all-gather.5.cloned.1.call-update
  8.8 0.0 reduce-scatter.2.cloned.1.call-start
  8.8 0.3 fusion.27
  9.2 0.8 fusion.30
  10.0 1.3 dynamic_slice.16
  13.8 0.0 copy-start.7
  13.8 0.0 copy-start.8
  13.8 0.0 copy-start.9
  13.8 8.9 copy.57
  22.7 0.0 copy-done.7
  22.7 0.0 copy-done.8
  22.7 0.0 copy-done.9
  22.7 0.4 convolution_bitcast_fusion.1
  23.1 0.2 copy.59
  23.2 0.3 copy.69
  23.5 0.1 broadcast_clamp_fusion
  23.7 865.7 %gather_fusion.2 = f32[262144,8]{1,0:T(8,128)} fusion(f32[8,640]{0,1:T(8,128)S(1)} %copy.59, s32[262144]{0:T(1024)S(1)} %broadcast_clamp_fusion), kind=kCustom, calls=%fused_computation.2 | custom fusion | bytes 17825792 | tf_op jit(solution)/shard_map/jit(_take)/gather | solution.py:65
  889.4 70.6 %copy.67 = f32[512,512,8]{1,0,2:T(8,128)} copy(f32[512,512,8]{2,1,0:T(8,128)} %bitcast.22) | data formatting | bytes 16777216 | tf_op jit(solution)/shard_map/jit(_take)/gather | solution.py:65
  959.9 0.0 copy-done.2
  959.9 0.1 copy.68
  960.1 217.0 %gather_fusion.1 = f32[65536,8]{1,0:T(8,128)} fusion(f32[8,640]{0,1:T(8,128)S(1)} %copy.59, s32[65536]{0:T(1024)S(1)} %broadcast_clamp_fusion.1), kind=kCustom, calls=%fused_computation.1 | custom fusion | bytes 4456448 | tf_op jit(solution)/shard_map/while/body/eval_jaxpr/cond/branch_1_fun/jit(_take)/gather | solution.py:65
  1177.1 20.1 %copy.66 = f32[128,512,8]{1,0,2:T(8,128)} copy(f32[128,512,8]{2,1,0:T(8,128)} %bitcast.95) | data formatting | bytes 4194304 | tf_op jit(solution)/shard_map/while/body/eval_jaxpr/cond/branch_1_fun/jit(_take)/gather | solution.py:65
  1197.9 0.0 copy-done.10
  1197.9 0.2 select_reduce_fusion
  1198.1 0.1 broadcast_in_dim.126
  1198.2 0.1 broadcast_in_dim.127
  1198.9 0.0 copy-done.11
  1198.9 0.6 dynamic_slice.17
  1199.5 0.6 iota_compare_fusion.2
  1200.2 0.8 fusion.31
  1201.0 1.5 subtract_compare_fusion
  1202.5 1.4 copy.54
  1203.9 0.6 gather_fusion
  1204.4 0.1 bitcast_select_fusion
  1204.6 0.1 copy.56
  1204.7 0.8 copy.61
  1205.5 2.1 fusion.3
  1207.5 6.9 convolution_convert_fusion
  1214.4 0.0 copy-start.3
  1214.5 1.1 fusion.43
  1215.6 1.3 copy.65
  1216.8 1.0 copy.62
  1217.8 1.3 copy.58
  1219.1 0.0 copy-done.3
  1219.1 0.0 copy-start.1
  1219.1 0.0 copy-start.4
  1219.1 0.0 copy-start.5
  1219.1 5.8 fusion.46
  1224.9 0.0 copy-done.1
  1224.9 0.0 copy-done.4
  1224.9 0.0 copy-done.5
  1224.9 0.8 fusion.45
  1225.7 1.2 fusion.1
  1226.9 1.4 fusion.16
  1228.3 0.3 fusion.14
  1228.7 0.6 fusion.23
  1229.3 2.6 select_convert_fusion
  1231.9 0.0 reduce-scatter.2.cloned.1.call-update
  1231.9 52.9 %reduce-scatter.2.cloned.1.call-done = bf16[128,2048]{1,0:T(8,128)(2,1)} async-done(((bf16[512,2048]{1,0:T(8,128)(2,1)}), bf16[128,2048]{1,0:T(8,128)(2,1)}) %reduce-scatter.2.cloned.1.call-update) | async-done | bytes 524304 | tf_op jit(solution)/shard_map/reduce_scatter | solution.py:139
  (19 shorter events, 0.1 us)
Async XLA Ops:
  6.5 1222.7 %copy-start = (bf16[512,2048]{1,0:T(8,128)(2,1)S(1)}, bf16[512,2048]{1,0:T(8,128)(2,1)}, u32[]{:S(2)}) copy-start(bf16[512,2048]{1,0:T(8,128)(2,1)} %param.13) | copy-start | bytes 6291460
  6.5 1196.0 %all-gather.3.cloned.1.call-start = ((), (), s32[]{:S(2)}) async-start(), calls=%async_computation.1 | async-start | bytes 1064960 | tf_op jit(solution)/shard_map/all_gather | solution.py:97
  8.0 1197.4 %all-gather.5.cloned.1.call-start = ((), (), s32[]{:S(2)}) async-start(), calls=%async_computation.2 | async-start | bytes 2621440 | tf_op jit(solution)/shard_map/all_gather | solution.py:40
  8.8 1276.0 %reduce-scatter.2.cloned.1.call-start = ((), (), s32[]{:S(2)}) async-start(), calls=%async_computation.3 | async-start | bytes 2621440 | tf_op jit(solution)/shard_map/reduce_scatter | solution.py:139
  13.8 8.9 copy-start.7
  13.8 8.9 copy-start.8
  13.8 8.9 copy-start.9
  889.4 70.6 %copy-start.2 = (s32[16,4,8,128]{3,2,1,0:T(8,128)S(1)}, s32[16,4,8,128]{3,2,1,0:T(8,128)}, u32[]{:S(2)}) copy-start(s32[16,4,8,128]{3,2,1,0:T(8,128)} %fusion.30) | copy-start | bytes 786436
  1177.1 20.8 %copy-start.10 = (s32[64]{0:T(128)S(1)}, s32[64]{0:T(128)}, u32[]{:S(2)}) copy-start(s32[64]{0:T(128)} %param.18) | copy-start | bytes 772
  1177.1 21.8 %copy-start.11 = (s32[64]{0:T(128)S(1)}, s32[64]{0:T(128)}, u32[]{:S(2)}) copy-start(s32[64]{0:T(128)} %param.16) | copy-start | bytes 772
  1214.4 4.6 copy-start.3
  1219.1 5.8 copy-start.1
  1219.1 5.8 copy-start.4
  1219.1 5.8 copy-start.5
  1226.9 1.8 copy-start.6
Sparse Core Ops, SparseCore 0:
  10.7 82.2 all-gather.2
  94.8 43.6 all-gather.4
  1232.0 52.7 reduce-scatter.1
where the time goes:
time: 1290 us
  local copies, waits for them, and re-layouts  1190 us (92%)
  waiting for transfers between devices  53.6 us (4%)
  matrix products  18.4 us (1%)
  between operations  17.3 us (1%)
    gather x4, local copies, waits for them, and re-layouts, attend(): jnp.take(bias_t, jnp.clip(distance, 0, dist_count - 1), axis=1)  1170 us
    reduce_scatter x1, waiting for transfers between devices, body(): lax.psum_scatter(jnp.where(alive[:, None], product, 0.0).astype(jnp.bfloa...  52.9 us
  transfers between devices with their start and end apart: 3, of which 1 were waited for; matrix products, arithmetic and copies ran while one was open for 92% of the time, Pallas kernels for 0%

commit v1 on v0

v1 whole, which is shorter than its diff:
```python
import functools

import jax
import jax.numpy as jnp
from jax import lax
from jax.experimental import pallas as pl
from jax.experimental.pallas import tpu as pltpu
from jax.sharding import PartitionSpec as P

MESH = pl.DeviceIdType.MESH
TP = 4
ROWS = 128
SLOT = ROWS * TP
D = 2048
COLS = 512
HEADS = 8
PB = 8
PREFIX = 128
DIST = 640
BUCKETS = 32
GROUPS = 4
GROUP_BLOCKS = 16
NEG = -1e30
CH = 4
CROWS = ROWS // CH


def position():
    s = lax.axis_index("seq")
    t = lax.axis_index("tp")
    return s // 16, lax.rem(s // 4, 4), lax.rem(s // 2, 2), lax.rem(s, 2), t


def place(x, y, zh, c, t):
    return (((x * 4 + y) * 2 + zh) * 2 + c, t)


def gather_kernel(hid, gain_ref, w_hbm, pref_ref, qkv_ref, pbuf, wv, hbuf, kvown, own_sem, w_sem, ss, rs, pss, prs):
    x, y, zh, c, t = position()
    zz = zh * 4 + t

    def along_z(step):
        other = lax.rem(zz + step + 8, 8)
        return place(x, y, other // 4, c, lax.rem(other, 4))

    right, left = along_z(1), along_z(-1)
    half = place(x, y, 1 - zh, c, t)
    xs = (place(lax.rem(x + 1, 4), y, zh, c, t), place(lax.rem(x + 3, 4), y, zh, c, t))
    ys = (place(x, lax.rem(y + 1, 4), zh, c, t), place(x, lax.rem(y + 3, 4), zh, c, t))
    core = place(x, y, zh, 1 - c, t)
    partners = (right, left, half, *xs, *ys, core)
    barrier = pltpu.get_barrier_semaphore()
    for partner in partners:
        pl.semaphore_signal(barrier, inc=1, device_id=partner, device_id_type=MESH)
    load_own = pltpu.make_async_copy(hid, hbuf.at[pl.ds(pl.multiple_of(t * ROWS, ROWS), ROWS)], own_sem.at[0])
    load_own.start()
    load_w = [pltpu.make_async_copy(w_hbm.at[i], wv.at[i], w_sem.at[i]) for i in range(3)]
    for copy in load_w:
        copy.start()
    both = pref_ref[...].astype(jnp.float32)
    kvown[0] = both[:, 0, :].astype(jnp.bfloat16)
    kvown[1] = both[:, 1, :].astype(jnp.bfloat16)
    pl.semaphore_wait(barrier, len(partners))

    def piece(shard, j):
        return pl.ds(pl.multiple_of(shard * ROWS + j * CROWS, CROWS), CROWS)

    def hop(way, k, j):
        shard = t - k if way == 0 else t + k
        source = hid.at[pl.ds(j * CROWS, CROWS)] if k == 0 else hbuf.at[piece(shard, j)]
        return pltpu.make_async_remote_copy(
            src_ref=source,
            dst_ref=hbuf.at[piece(shard, j)],
            send_sem=ss.at[way, k, j],
            recv_sem=rs.at[way, k, j],
            device_id=right if way == 0 else left,
            device_id_type=MESH,
        )

    def sends(way, k):
        return (t < TP - 1) & (t - k >= 0) if way == 0 else (t > 0) & (t + k < TP)

    def gets(way, k):
        return t - k >= 0 if way == 0 else t + k < TP

    for j in range(CH):
        for way in range(2):
            @pl.when(sends(way, 0))
            def _():
                hop(way, 0, j).start()

    def remote(index, src, dst, to):
        return pltpu.make_async_remote_copy(
            src_ref=src, dst_ref=dst, send_sem=pss.at[index], recv_sem=prs.at[index], device_id=to, device_id_type=MESH
        )

    mine = pbuf.at[c, y, x, zh]
    local = pltpu.make_async_copy(kvown, mine, own_sem.at[1])
    local.start()
    swap = remote(0, kvown, mine, half)
    swap.start()

    def ring(base, view, part, me, peers):
        ahead, behind = lax.rem(me + 1, 4), lax.rem(me + 3, 4)

        def first():
            for k in range(2):
                remote(base + k, view(me), view(me), peers[k]).start()

        def arrived():
            remote(base, view(behind), view(behind), peers[0]).wait_recv()
            remote(base + 1, view(ahead), view(ahead), peers[1]).wait_recv()

        def second():
            remote(base + 2, part(behind, 0), part(behind, 0), peers[0]).start()
            remote(base + 3, part(ahead, 1), part(ahead, 1), peers[1]).start()

        def complete():
            far = lax.rem(me + 2, 4)
            remote(base + 2, part(far, 0), part(far, 0), peers[0]).wait_recv()
            remote(base + 3, part(far, 1), part(far, 1), peers[1]).wait_recv()

        def drain():
            for k in range(2):
                remote(base + k, view(me), view(me), peers[k]).wait_send()
            remote(base + 2, part(behind, 0), part(behind, 0), peers[0]).wait_send()
            remote(base + 3, part(ahead, 1), part(ahead, 1), peers[1]).wait_send()

        return first, arrived, second, complete, drain

    ring_x = ring(1, lambda i: pbuf.at[c, y, i], lambda i, h: pbuf.at[c, y, i, h], x, xs)
    ring_y = ring(5, lambda i: pbuf.at[c, i], lambda i, h: pbuf.at[c, i, pl.ds(2 * h, 2)], y, ys)
    swap_core = remote(9, pbuf.at[c], pbuf.at[c], core)

    def project(shard):
        rows = pl.ds(pl.multiple_of(shard * ROWS, ROWS), ROWS)
        states = hbuf[rows, :].astype(jnp.float32)
        scale = lax.rsqrt(jnp.mean(states * states, -1, keepdims=True) + 1e-06)
        normed = (states * scale * gain_ref[...].astype(jnp.float32)).astype(jnp.bfloat16)
        for i in range(3):
            qkv_ref[rows, i * COLS : (i + 1) * COLS] = jnp.dot(
                normed, wv[i], preferred_element_type=jnp.float32
            ).astype(jnp.bfloat16)

    def pass_on(k, j):
        for way in range(2):
            @pl.when(gets(way, k))
            def _():
                shard = t - k if way == 0 else t + k
                pltpu.make_async_remote_copy(
                    src_ref=hbuf.at[piece(shard, j)],
                    dst_ref=hbuf.at[piece(shard, j)],
                    send_sem=ss.at[way, k - 1, j],
                    recv_sem=rs.at[way, k - 1, j],
                    device_id=right if way == 0 else left,
                    device_id_type=MESH,
                ).wait_recv()

            @pl.when(sends(way, k))
            def _():
                hop(way, k, j).start()

    def order(i):
        ends = jnp.where(t == 0, i, TP - 1 - i)
        inner = jnp.where(t == 1, (0, 2, 3)[i - 1], (3, 1, 0)[i - 1])
        return jnp.where((t == 0) | (t == TP - 1), ends, inner)

    load_own.wait()
    for copy in load_w:
        copy.wait()
    project(t)
    swap.wait_recv()
    local.wait()
    ring_x[0]()
    pass_on(1, 0)
    ring_x[1]()
    ring_x[2]()
    pass_on(1, 1)
    ring_x[3]()
    ring_y[0]()
    pass_on(1, 2)
    pass_on(1, 3)
    ring_y[1]()
    ring_y[2]()
    project(order(1))
    pass_on(2, 0)
    ring_y[3]()
    swap_core.start()
    pass_on(2, 1)
    pass_on(2, 2)
    pass_on(2, 3)
    project(order(2))
    for j in range(CH):
        pass_on(3, j)
    project(order(3))
    remote(9, pbuf.at[1 - c], pbuf.at[1 - c], core).wait_recv()
    swap.wait_send()
    ring_x[4]()
    ring_y[4]()
    swap_core.wait_send()
    for k in range(TP):
        for j in range(CH):
            for way in range(2):
                if k == TP - 1:
                    continue

                @pl.when(sends(way, k))
                def _():
                    hop(way, k, j).wait_send()


def gather(hidden, gain, weights, prefix):
    vmem, hbm = pl.BlockSpec(memory_space=pltpu.VMEM), pl.BlockSpec(memory_space=pl.ANY)
    return pl.pallas_call(
        gather_kernel,
        name="gather",
        out_shape=(
            jax.ShapeDtypeStruct((SLOT, 3 * COLS), jnp.bfloat16),
            jax.ShapeDtypeStruct((2, 4, 4, 2, 2, PB, COLS), jnp.bfloat16),
        ),
        in_specs=[hbm, vmem, hbm, vmem],
        out_specs=(vmem, hbm),
        scratch_shapes=[
            pltpu.VMEM((3, D, COLS), jnp.bfloat16),
            pltpu.VMEM((SLOT, D), jnp.bfloat16),
            pltpu.VMEM((2, PB, COLS), jnp.bfloat16),
            pltpu.SemaphoreType.DMA((2,)),
            pltpu.SemaphoreType.DMA((3,)),
            pltpu.SemaphoreType.DMA((2, TP, CH)),
            pltpu.SemaphoreType.DMA((2, TP, CH)),
            pltpu.SemaphoreType.DMA((10,)),
            pltpu.SemaphoreType.DMA((10,)),
        ],
        compiler_params=pltpu.CompilerParams(collective_id=0, has_side_effects=True, vmem_limit_bytes=48 << 20),
    )(hidden, gain, weights, prefix)


def attention_kernel(request_ref, block_ref, qkv_ref, pbuf, bucket_ref, table_ref, attn_ref, inverse, pre, bias, tiles, sem):
    s = lax.axis_index("seq")
    group = request_ref[s] // GROUP_BLOCKS

    def note(i, carry):
        inverse[block_ref[i]] = i
        return carry

    lax.fori_loop(0, GROUPS * GROUP_BLOCKS, note, 0)
    copies = []
    for j in range(GROUP_BLOCKS):
        owner = inverse[group * GROUP_BLOCKS + j]
        c, zh, y, x = lax.rem(owner, 2), lax.rem(owner // 2, 2), lax.rem(owner // 4, 4), owner // 16
        copy = pltpu.make_async_copy(pbuf.at[((c * 4 + y) * 4 + x) * 2 + zh], pre.at[j], sem.at[j])
        copy.start()
        copies.append(copy)

    bucket = jnp.broadcast_to(bucket_ref[...], (HEADS, DIST))
    row = jnp.zeros((HEADS, DIST), jnp.float32)
    for b in range(BUCKETS):
        row = jnp.where(bucket == b, table_ref[:, b : b + 1], row)
    bias[:, :PREFIX] = jnp.full((HEADS, PREFIX), NEG, jnp.float32)
    bias[:, PREFIX:] = row
    for h in range(HEADS):
        for delta in range(5):
            window = jnp.broadcast_to(bias[h : h + 1, delta * 128 : delta * 128 + 256], (128, 256))
            rolled = pltpu.roll(window, 0, 1, stride=1, stride_axis=0)
            tiles[h // 2, delta, :, (h % 2) * 128 : (h % 2) * 128 + 128] = rolled[:, 128:]
    for copy in copies:
        copy.wait()

    low = lax.broadcasted_iota(jnp.int32, (128, 128), 1) < 64
    for p in range(HEADS // 2):
        lanes = slice(p * 128, p * 128 + 128)

        def prefix(which):
            parts = [pre[j, which, :, lanes].astype(jnp.float32) for j in range(GROUP_BLOCKS)]
            return jnp.concatenate(parts, 0).astype(jnp.bfloat16)

        keys = jnp.concatenate([prefix(0), qkv_ref[:, COLS + p * 128 : COLS + p * 128 + 128]], 0)
        values = jnp.concatenate([prefix(1), qkv_ref[:, 2 * COLS + p * 128 : 2 * COLS + p * 128 + 128]], 0)
        values_t = values.T
        for r in range(TP):
            query = qkv_ref[r * 128 : r * 128 + 128, lanes]
            zero = jnp.zeros_like(query)
            stacked = jnp.concatenate([jnp.where(low, query, zero), jnp.where(low, zero, query)], 0)
            blocks = []
            for kb in range(r + 2):
                part = lax.dot_general(
                    keys[kb * 128 : kb * 128 + 128], stacked, (((1,), (1,)), ((), ())), preferred_element_type=jnp.float32
                )
                blocks.append(part + tiles[p, r + 1 - kb])
            top = functools.reduce(jnp.maximum, [jnp.max(b, 0, keepdims=True) for b in blocks])
            probs = [jnp.exp(b - top) for b in blocks]
            denom = functools.reduce(jnp.add, [jnp.sum(b, 0, keepdims=True) for b in probs])
            probs = jnp.concatenate([b.astype(jnp.bfloat16) for b in probs], 0)
            out = jnp.dot(values_t[:, : (r + 2) * 128], probs, preferred_element_type=jnp.float32) / denom
            pair = jnp.concatenate([out[:64, :128], out[64:, 128:]], 0)
            attn_ref[r * 128 : r * 128 + 128, lanes] = pair.T.astype(jnp.bfloat16)


def attention(request_of_slot, block_of_slot, qkv, pbuf, bucket, table):
    vmem, hbm = pl.BlockSpec(memory_space=pltpu.VMEM), pl.BlockSpec(memory_space=pl.ANY)
    smem = pl.BlockSpec(memory_space=pltpu.SMEM)
    return pl.pallas_call(
        attention_kernel,
        name="attention",
        out_shape=jax.ShapeDtypeStruct((SLOT, COLS), jnp.bfloat16),
        in_specs=[smem, smem, vmem, hbm, vmem, vmem],
        out_specs=vmem,
        scratch_shapes=[
            pltpu.SMEM((GROUPS * GROUP_BLOCKS,), jnp.int32),
            pltpu.VMEM((GROUP_BLOCKS, 2, PB, COLS), jnp.bfloat16),
            pltpu.VMEM((HEADS, PREFIX + DIST), jnp.float32),
            pltpu.VMEM((HEADS // 2, 5, 128, 256), jnp.float32),
            pltpu.SemaphoreType.DMA((GROUP_BLOCKS,)),
        ],
        compiler_params=pltpu.CompilerParams(vmem_limit_bytes=48 << 20),
    )(request_of_slot, block_of_slot, qkv, pbuf, bucket, table)


def body(
    hidden,
    norm_gain,
    qkv_weight,
    out_weight,
    bias_table,
    prefix_cache,
    suffix_lengths,
    request_of_slot,
    block_of_slot,
    bias_bucket,
):
    request = lax.dynamic_index_in_dim(request_of_slot, lax.axis_index("seq"), 0, keepdims=False)
    length = lax.dynamic_index_in_dim(suffix_lengths, request, 0, keepdims=False)
    qkv, pbuf = gather(hidden[0], norm_gain[None], qkv_weight.transpose(1, 0, 2), prefix_cache)
    attn = attention(
        request_of_slot, block_of_slot, qkv, pbuf.reshape(64, 2, PB, COLS), bias_bucket[None], bias_table.T
    )
    product = jnp.dot(attn, out_weight, preferred_element_type=jnp.float32)
    alive = jnp.arange(SLOT, dtype=jnp.int32) < length
    summed = lax.psum_scatter(
        jnp.where(alive[:, None], product, 0.0).astype(jnp.bfloat16),
        "tp",
        scatter_dimension=0,
        tiled=True,
    )
    return summed[None]


def solution(mesh):
    return jax.shard_map(
        body,
        mesh=mesh,
        in_specs=(
            P("seq", "tp", None),
            P(),
            P(None, None, "tp"),
            P("tp", None),
            P(None, "tp"),
            P("seq", None, "tp"),
            P(),
            P(),
            P(),
            P(),
        ),
        out_specs=P("seq", "tp", None),
        check_vma=False,
    )
```

time: 1290 us -> 130 us (0.10)
  local copies, waits for them, and re-layouts: 1190 us -> 5.78 us
  Pallas kernels: 0 us -> 54.4 us
  matrix products: 18.4 us -> 2.62 us
    gather x5 -> x0, local copies, waits for them, and re-layouts: 1170 us -> none  [the longest x4 1170 us: attend(): jnp.take(bias_t, jnp.clip(distance, 0, dist_count - 1), axis=1)]
    pallas_call x0 -> x2, Pallas kernels: none -> 54.4 us  [the longest x1 46.1 us: gather(): pl.pallas_call(gather_kernel, name='gather', out_shape=(jax.ShapeDtypeStr...]
    dot_general x6 -> x0, matrix products: 15.8 us -> none  [the longest x1 6.89 us: body(): jnp.dot(normed, weights, preferred_element_type=jnp.float32)]
  transfers between devices with their start and end apart: 3 -> 1, of which waited for: 1 -> 1; matrix products, arithmetic and copies ran while one was open for 92% -> 0% of each run, Pallas kernels for 0% -> 0%
where the time goes in v1:
time: 130 us; the launch traced here: 129 us
  Pallas kernels  54.4 us (42%)
  waiting for transfers between devices  50.6 us (39%)
  between operations  15.4 us (12%)
  local copies, waits for them, and re-layouts  5.78 us (4%)
  matrix products  2.62 us (2%)
    reduce_scatter x1, waiting for transfers between devices, body(): lax.psum_scatter(jnp.where(alive[:, None], product, 0.0).astype(jnp.bfloa...  50.6 us
    pallas_call x1, Pallas kernels, gather(): pl.pallas_call(gather_kernel, name='gather', out_shape=(jax.ShapeDtypeStr...  46.1 us
    pallas_call x1, Pallas kernels, attention(): pl.pallas_call(attention_kernel, name='attention', out_shape=jax.ShapeDty...  8.36 us
    dot_general x1, matrix products, body(): product = jnp.dot(attn, out_weight, preferred_element_type=jnp.float32)  2.62 us
  transfers between devices with their start and end apart: 1, of which 1 were waited for; matrix products, arithmetic and copies ran while one was open for 0% of the time, Pallas kernels for 0%

profile of v1, /device:TPU:1, one launch (start us, length us, event | category | flops | bytes accessed | tf_op | source)
XLA Modules:
  0.0 129.4 jit_solution(13233465682065009623)
XLA Ops:
  6.5 0.0 copy-start
  6.5 0.0 reduce-scatter.2.cloned.1.call-start
  6.5 1.4 %dynamic_slice.7 = s32[1]{0:T(128)} dynamic-slice(s32[64]{0:T(128)} %request_ref.1, s32[]{:T(128)S(6)} %select_n.11), dynamic_slice_sizes={1} | dynamic-slice | bytes 12 | tf_op jit(solution)/shard_map/jit(dynamic_index_in_dim)/dynamic_slice | solution.py:331
  9.2 0.7 broadcast_in_dim.23.gain_ref
  9.9 0.7 broadcast_in_dim.24.bucket_ref
  11.3 1.2 dynamic_slice.8
  12.5 0.6 iota_compare_fusion
  13.2 0.0 copy-start.1
  13.2 1.0 copy-done.1
  14.2 0.0 copy-start.2
  14.2 0.7 copy-done.2
  14.9 0.0 copy-start.3
  14.9 0.0 copy-start.4
  14.9 0.0 copy-start.5
  14.9 46.1 %gather.1 = (bf16[512,1536]{1,0:T(8,128)(2,1)S(1)}, bf16[2,4,4,2,2,8,512]{6,5,4,3,2,1,0:T(8,128)(2,1)S(1)}) custom-call(bf16[128,2048]{1,0:T(8,128)(2,1)S(1)} %bitcast.10, bf16[1,2048]{1,0:T(2,128)(2,1)S(1)} %broadcast_in_dim.23.gain_ref, bf16[3,2048,512]{2,1,0:T(8,128)(2,1)} %bitcast.12, bf16[8,2,512]{2,1,0:T(2,128)(2,1)S(1)} %copy-done.2), custom_call_target="tpu_custom_call" | custom-call | tf_op jit(solution)/shard_map/gather/pallas_call | solution.py:214
  61.0 0.0 copy-done.3
  61.0 0.0 copy-done.4
  61.0 0.0 copy-done.5
  61.0 8.4 %attention.1 = bf16[512,512]{1,0:T(8,128)(2,1)S(1)} custom-call(s32[64]{0:T(128)S(1)} %copy-done.4, s32[64]{0:T(128)S(1)} %copy-done.5, bf16[512,1536]{1,0:T(8,128)(2,1)S(1)} %get-tuple-element.7.qkv_ref, bf16[64,2,8,512]{3,2,1,0:T(8,128)(2,1)S(1)} %bitcast.9, s32[1,640]{1,0:T(1,128)S(1)} %broadcast_in_dim.24.bucket_ref, f32[8,32]{1,0:T(8,128)S(1)} %bitcast.11), custom_call_target="tpu_custom_call" | custom-call | tf_op jit(solution)/shard_map/attention/pallas_call | solution.py:302
  69.4 0.0 copy-done
  69.4 2.6 %select_convert_fusion = bf16[512,2048]{1,0:T(8,128)(2,1)} fusion(bf16[512,512]{1,0:T(8,128)(2,1)S(1)} %attention.1, bf16[512,2048]{1,0:T(8,128)(2,1)S(1)} %copy-done, pred[512]{0:T(512)(128)(4,1)S(1)} %iota_compare_fusion), kind=kOutput, calls=%fused_computation | convolution fusion | flops 1075838976 | bytes 4719104 | tf_op jit(solution)/shard_map/dot_general | solution.py:337
  72.0 0.0 reduce-scatter.2.cloned.1.call-update
  72.0 50.6 %reduce-scatter.2.cloned.1.call-done = bf16[128,2048]{1,0:T(8,128)(2,1)} async-done(((bf16[512,2048]{1,0:T(8,128)(2,1)}), bf16[128,2048]{1,0:T(8,128)(2,1)}) %reduce-scatter.2.cloned.1.call-update) | async-done | bytes 524304 | tf_op jit(solution)/shard_map/reduce_scatter | solution.py:339
Async XLA Ops:
  6.5 62.9 %copy-start = (bf16[512,2048]{1,0:T(8,128)(2,1)S(1)}, bf16[512,2048]{1,0:T(8,128)(2,1)}, u32[]{:S(2)}) copy-start(bf16[512,2048]{1,0:T(8,128)(2,1)} %param.13) | copy-start | bytes 6291460
  6.5 116.1 %reduce-scatter.2.cloned.1.call-start = ((), (), s32[]{:S(2)}) async-start(), calls=%async_computation.1 | async-start | bytes 2621440 | tf_op jit(solution)/shard_map/reduce_scatter | solution.py:339
  13.2 1.0 copy-start.1
  14.2 0.7 copy-start.2
  14.9 46.1 %copy-start.3 = (f32[32,8]{0,1:T(8,128)S(1)}, f32[32,8]{0,1:T(8,128)}, u32[]{:S(2)}) copy-start(f32[32,8]{0,1:T(8,128)} %param.14) | copy-start | bytes 3076
  14.9 46.1 %copy-start.4 = (s32[64]{0:T(128)S(1)}, s32[64]{0:T(128)}, u32[]{:S(2)}) copy-start(s32[64]{0:T(128)} %request_ref.1) | copy-start | bytes 772
  14.9 46.1 %copy-start.5 = (s32[64]{0:T(128)S(1)}, s32[64]{0:T(128)}, u32[]{:S(2)}) copy-start(s32[64]{0:T(128)} %block_ref.1) | copy-start | bytes 772
Sparse Core Ops, SparseCore 0:
  72.2 50.3 reduce-scatter.1

commit v2 on v0

v2 whole, which is shorter than its diff:
```python
import functools

import jax
import jax.numpy as jnp
from jax import lax
from jax.experimental import pallas as pl
from jax.experimental.pallas import tpu as pltpu
from jax.sharding import PartitionSpec as P

MESH = pl.DeviceIdType.MESH
TP = 4
ROWS = 128
SLOT = ROWS * TP
D = 2048
COLS = 512
HEADS = 8
PB = 8
PREFIX = 128
CACHE = 512
DIST = 640
BUCKETS = 32
RG = 16
NEG = -1e30
CH = 4
CROWS = ROWS // CH


def aligned(start, unit):
    return pl.multiple_of(start, unit)


def remote(src, dst, send_sem, recv_sem, to):
    return pltpu.make_async_remote_copy(
        src_ref=src, dst_ref=dst, send_sem=send_sem, recv_sem=recv_sem, device_id=to, device_id_type=MESH
    )


class Track:
    def __init__(self, view, columns, off, unit, me, peers, send, recv):
        self.view, self.columns, self.off, self.unit = view, columns, off, unit
        self.me, self.peers, self.send, self.recv = me, peers, send, recv

    def region(self, stage, i, part=None):
        count = self.unit if stage == 0 else 4 * self.unit
        start = self.off + (self.me[1] * 4 * self.unit + i * self.unit if stage == 0 else i * 4 * self.unit)
        half = self.columns // 2
        columns = pl.ds(0, self.columns) if part is None else pl.ds(part * half, half)
        return self.view(pl.ds(aligned(start, self.unit), count), columns)

    def copy(self, stage, k, i):
        region = self.region(stage, i, None if k < 2 else k - 2)
        return remote(region, region, self.send.at[stage, k], self.recv.at[stage, k], self.peers[stage][k % 2])

    def near(self, stage):
        me = self.me[stage]
        return lax.rem(me + 3, 4), lax.rem(me + 1, 4), lax.rem(me + 2, 4)

    def first(self, stage):
        for k in range(2):
            self.copy(stage, k, self.me[stage]).start()

    def second(self, stage):
        behind, ahead, _ = self.near(stage)
        self.copy(stage, 0, behind).wait_recv()
        self.copy(stage, 1, ahead).wait_recv()
        self.copy(stage, 2, behind).start()
        self.copy(stage, 3, ahead).start()

    def complete(self, stage):
        far = self.near(stage)[2]
        self.copy(stage, 2, far).wait_recv()
        self.copy(stage, 3, far).wait_recv()

    def drain(self):
        for stage in range(2):
            behind, ahead, _ = self.near(stage)
            for k, i in enumerate((self.me[stage], self.me[stage], behind, ahead)):
                self.copy(stage, k, i).wait_send()


def kernel(
    request_ref, block_ref, length_ref, hid, gain_ref, w_hbm, pref, wo_hbm, bucket_ref, table_ref, out_ref,
    wbuf, hbuf, nbuf, acc, qkv, prefv, kvown, pbuf, tab, bias, tiles, wo, won, asend, aall,
    loc, own_s, sib_s, fwd_s, h_r, wz_s, wz_r, tb_s, tb_r, pz_s, pz_r, oz_s, oz_r,
    wt_s, wt_r, pt_s, pt_r, ot_s, ot_r, wc_s, wc_r, oc_s, oc_r, at_s, at_r,
):
    s = lax.axis_index("seq")
    t = lax.axis_index("tp")
    x, y, zh, c = s // 16, lax.rem(s // 4, 4), lax.rem(s // 2, 2), lax.rem(s, 2)
    side = t // 2
    leader = c == side
    inner = (t == 1) | (t == 2)
    beside = t + 1 - 2 * lax.rem(t, 2)
    across = lax.rem(t + 2, 4)
    group = lax.rem(t, 2) + 2 * c

    def at(zh_, c_, t_):
        return (((x * 4 + y) * 2 + zh_) * 2 + c_, t_)

    def column(x_, y_):
        return (((x_ * 4 + y_) * 2 + zh) * 2 + c, t)

    def along(step):
        other = lax.rem(zh * 4 + t + step + 8, 8)
        return at(other // 4, c, lax.rem(other, 4))

    xs = (column(lax.rem(x + 1, 4), y), column(lax.rem(x + 3, 4), y))
    ys = (column(x, lax.rem(y + 1, 4)), column(x, lax.rem(y + 3, 4)))
    core = at(zh, 1 - c, t)

    partners = [at(zh, lax.rem(c + dc, 2), lax.rem(t + dt, 4)) for dt in range(4) for dc in range(2) if dt or dc]
    partners += [at(1 - zh, c_, t_) for t_ in (t, across) for c_ in (c, 1 - c)]
    partners += [*xs, *ys]
    barrier = pltpu.get_barrier_semaphore()
    for partner in partners:
        pl.semaphore_signal(barrier, inc=1, device_id=partner, device_id_type=MESH)

    load_pref = pltpu.make_async_copy(pref, prefv, loc.at[0])
    load_pref.start()
    load_own = pltpu.make_async_copy(hid, hbuf.at[pl.ds(aligned(t * ROWS, ROWS), ROWS)], loc.at[1])

    @pl.when(leader)
    def _():
        load_own.start()

    load_w = pltpu.make_async_copy(w_hbm, wbuf.at[0], loc.at[2])
    load_w.start()
    load_wo = pltpu.make_async_copy(wo_hbm, won, loc.at[3])
    load_wo.start()
    load_pref.wait()
    both = prefv[...].astype(jnp.float32)
    kvown[0] = both[:, 0, :].astype(jnp.bfloat16)
    kvown[1] = both[:, 1, :].astype(jnp.bfloat16)
    pl.semaphore_wait(barrier, len(partners))

    def prefix_row(kv, zh_, c_):
        place = (y * 4 + x) if kv == 0 else (x * 4 + y)
        return pl.ds(aligned((place * 4 + zh_ * 2 + c_) * PB, PB), PB)

    def prefix_copy(target, kv, zh_, c_, to):
        rows = prefix_row(kv, zh_, c_)
        return remote(kvown.at[kv], pbuf.at[kv, rows], pz_s.at[target, kv], pz_r.at[zh_ * 2 + c_, kv], to)

    readers = (at(1 - zh, side, t), at(zh, side, across), at(1 - zh, side, across))
    own_prefix = [
        pltpu.make_async_copy(kvown.at[kv], pbuf.at[kv, prefix_row(kv, zh, c)], loc.at[4 + kv]) for kv in range(2)
    ]
    for kv in range(2):
        for k, reader in enumerate(readers):
            prefix_copy(k, kv, zh, c, reader).start()

        @pl.when(leader)
        def _():
            own_prefix[kv].start()

        @pl.when(jnp.logical_not(leader))
        def _():
            prefix_copy(3, kv, zh, c, core).start()

    send_table = remote(table_ref, tab, tb_s.at[0], tb_r.at[0], at(zh, c, across))
    send_table.start()

    def weight_row(hh):
        return hh * 1024 + c * 512 + ((y * 4 + x) if hh == 0 else (x * 4 + y)) * 32

    def weight_piece(hh):
        rows = pl.ds(aligned(weight_row(hh), 32), 32)
        return remote(
            w_hbm.at[:, rows], wbuf.at[1, :, rows], wz_s.at[hh], wz_r.at[hh], along(2 if hh == 0 else -2)
        )

    for hh in range(2):
        weight_piece(hh).start()

    def quarter(k):
        j = jnp.where(t < 2, 2, 1)
        f = jnp.where(t < 2, 3, 0)
        return (t, beside, j, f)[k]

    def chunk(q, j):
        return hbuf.at[pl.ds(aligned(q * ROWS + j * CROWS, CROWS), CROWS)]

    own_to = at(zh, c, jnp.where(leader, beside, quarter(2)))

    def own_copy(j):
        return remote(hid.at[pl.ds(j * CROWS, CROWS)], chunk(t, j), own_s.at[j], h_r.at[t, j], own_to)

    def sibling_copy(k, j):
        q = quarter(k)
        src = hid.at[pl.ds(j * CROWS, CROWS)] if k == 0 else chunk(q, j)
        return remote(src, chunk(q, j), sib_s.at[k, j], h_r.at[q, j], core)

    def forward_copy(k, j):
        q = quarter(k)
        return remote(chunk(q, j), chunk(q, j), fwd_s.at[k, j], h_r.at[q, j], at(zh, c, beside))

    for j in range(CH):
        own_copy(j).start()

    for j in range(CH):
        @pl.when(leader)
        def _():
            sibling_copy(0, j).start()

    def out_row(hh):
        return hh * 256 + c * 128 + ((y * 4 + x) if hh == 0 else (x * 4 + y)) * 8

    def out_piece(d, hh):
        rows = pl.ds(aligned(out_row(hh), 8), 8)
        return remote(
            wo_hbm.at[rows], wo.at[3 - d, rows], oz_s.at[d - 1, hh], oz_r.at[3 - d, hh], at(zh, c, lax.rem(t + d, 4))
        )

    def arrive(k, j):
        if k == 0:
            @pl.when(jnp.logical_not(leader))
            def _():
                sibling_copy(0, j).wait_recv()
        else:
            sibling_copy(k, j).wait_recv()

            @pl.when(leader)
            def _():
                sibling_copy(k, j).start()

            if k >= 2:
                @pl.when(leader & inner)
                def _():
                    forward_copy(k, j).start()

    def tracks(views, columns, offs, unit, send, recv):
        first = Track(views[0], columns, offs[0], unit, (x, y), (xs, ys), send.at[0], recv.at[0])
        other = Track(views[1], columns, offs[1], unit, (y, x), (ys, xs), send.at[1], recv.at[1])
        return first, other

    w_view = lambda rows, columns: wbuf.at[1, :, rows, columns]
    o_view = lambda rows, columns: wo.at[:, rows, columns]
    w_tracks = tracks((w_view, w_view), COLS, (c * 512, 1024 + c * 512), 32, wt_s, wt_r)
    p_tracks = tracks(
        (lambda rows, columns: pbuf.at[0, rows, columns], lambda rows, columns: pbuf.at[1, rows, columns]),
        COLS, (0, 0), 32, pt_s, pt_r,
    )
    o_tracks = tracks((o_view, o_view), D, (c * 128, 256 + c * 128), 8, ot_s, ot_r)

    def core_weights(hh, i, core_):
        start = hh * 1024 + core_ * 512 + i * 128
        region = wbuf.at[1, :, pl.ds(aligned(start, 128), 128)]
        return remote(region, region, wc_s.at[hh, i], wc_r.at[hh, i], core)

    def core_out(hh, core_):
        region = wo.at[:, pl.ds(aligned(hh * 256 + core_ * 128, 128), 128)]
        return remote(region, region, oc_s.at[hh], oc_r.at[hh], core)

    def each(which, action, stage):
        for track in which:
            getattr(track, action)(stage)

    def norm(k):
        rows = pl.ds(aligned(quarter(k) * ROWS, ROWS), ROWS)
        gain = jnp.concatenate([gain_ref[i : i + 1, :].astype(jnp.float32) for i in range(D // 128)], 1)
        states = hbuf[rows, :].astype(jnp.float32)
        scale = lax.rsqrt(jnp.mean(states * states, -1, keepdims=True) + 1e-06)
        nbuf[rows, :] = (states * scale * gain).astype(jnp.bfloat16)

    for kv in range(2):
        for zh_ in range(2):
            for c_ in range(2):
                mine = leader & (zh == zh_) & (c == c_)

                @pl.when(jnp.logical_not(mine))
                def _():
                    prefix_copy(0, kv, zh_, c_, core).wait_recv()

        @pl.when(leader)
        def _():
            own_prefix[kv].wait()

    each(p_tracks, "first", 0)
    send_table.wait_recv()

    for j in range(2):
        arrive(0, j)
        arrive(1, j)
    for hh in range(2):
        weight_piece(hh).wait_recv()
    each(w_tracks, "first", 0)
    each(p_tracks, "second", 0)
    for d in range(1, 4):
        for hh in range(2):
            out_piece(d, hh).start()
    each(w_tracks, "second", 0)
    for j in range(2, CH):
        arrive(0, j)
        arrive(1, j)
    each(w_tracks, "complete", 0)
    each(w_tracks, "first", 1)
    each(p_tracks, "complete", 0)
    each(p_tracks, "first", 1)

    bucket = jnp.concatenate([bucket_ref[i : i + 1, :] for i in range(DIST // 128)], 1)
    bucket = jnp.broadcast_to(bucket, (HEADS, DIST))
    table = jnp.where(leader, table_ref[...], tab[...])
    row = jnp.zeros((HEADS, DIST), jnp.float32)
    for b in range(BUCKETS):
        row = jnp.where(bucket == b, table[:, b : b + 1], row)
    bias[:, :PREFIX] = jnp.full((HEADS, PREFIX), NEG, jnp.float32)
    bias[:, PREFIX:] = row

    def build(h):
        for delta in range(5):
            window = jnp.broadcast_to(bias[h : h + 1, delta * 128 : delta * 128 + 256], (128, 256))
            rolled = pltpu.roll(window, 0, 1, stride=1, stride_axis=0)
            tiles[h // 2, delta, :, (h % 2) * 128 : (h % 2) * 128 + 128] = rolled[:, 128:]

    for j in range(CH):
        arrive(2, j)
        build(j)
    each(p_tracks, "second", 1)
    for rho in range(3):
        for hh in range(2):
            out_piece(3 - rho, hh).wait_recv()
    each(o_tracks, "first", 0)

    @pl.when(leader)
    def _():
        load_own.wait()

    norm(0)
    each(o_tracks, "second", 0)
    for j in range(CH):
        arrive(3, j)
        build(CH + j)
    norm(1)
    each(w_tracks, "second", 1)
    each(o_tracks, "complete", 0)

    @pl.when(leader)
    def _():
        for hh, me in ((0, y), (1, x)):
            for i in (me, lax.rem(me + 1, 4), lax.rem(me + 3, 4)):
                core_weights(hh, i, c).start()

    norm(2)
    norm(3)
    each(p_tracks, "complete", 1)
    each(w_tracks, "complete", 1)
    each(o_tracks, "first", 1)

    @pl.when(leader)
    def _():
        for hh, me in ((0, y), (1, x)):
            core_weights(hh, lax.rem(me + 2, 4), c).start()

    load_w.wait()
    which = jnp.where(leader, 0, 1)
    for step, (hh, core_) in enumerate(((0, c), (1, c), (0, 1 - c), (1, 1 - c))):
        if step >= 2:
            @pl.when(jnp.logical_not(leader))
            def _():
                for i in range(4):
                    core_weights(hh, i, core_).wait_recv()

        rows = pl.ds(aligned(hh * 1024 + core_ * 512, 512), 512)
        for i in range(3):
            columns = slice(i * COLS, (i + 1) * COLS)
            part = jnp.dot(nbuf[:, rows], wbuf[which, i, rows, :], preferred_element_type=jnp.float32)
            if step == 0:
                acc[:, columns] = part
            elif step < 3:
                acc[:, columns] += part
            else:
                qkv[:, columns] = (acc[:, columns] + part).astype(jnp.bfloat16)

    slot = ((x * 4 + y) * 2 + zh) * 2 + side
    first_row = request_ref[slot] // RG * PREFIX
    lane = lax.broadcasted_iota(jnp.int32, (1, CACHE), 1)
    chosen = []
    for kv in range(2):
        target = jnp.zeros((1, CACHE), jnp.int32)
        for place in range(CACHE // PB):
            owner = (place // 4 % 4 * 4 + place // 16) * 4 + place % 4 if kv == 0 else place
            target = jnp.where(lane // PB == place, block_ref[owner] * PB, target)
        target = target + lane % PB - first_row
        match = lax.broadcasted_iota(jnp.int32, (PREFIX, CACHE), 0) == jnp.broadcast_to(target, (PREFIX, CACHE))
        pick = jnp.where(match, 1.0, 0.0).astype(jnp.bfloat16)
        chosen.append(jnp.dot(pick, pbuf[kv], preferred_element_type=jnp.float32).astype(jnp.bfloat16))

    low = lax.broadcasted_iota(jnp.int32, (128, 128), 1) < 64
    keys, values = [], []
    for p in range(HEADS // 2):
        lanes = slice(p * 128, p * 128 + 128)
        keys.append(chosen[0][:, lanes])
        values.append(
            jnp.concatenate([chosen[1][:, lanes], qkv[:, 2 * COLS + p * 128 : 2 * COLS + p * 128 + 128]], 0).T
        )

    def attend(r):
        for p in range(HEADS // 2):
            lanes = slice(p * 128, p * 128 + 128)
            query = qkv[r * 128 : r * 128 + 128, lanes]
            zero = jnp.zeros_like(query)
            stacked = jnp.concatenate([jnp.where(low, query, zero), jnp.where(low, zero, query)], 0)
            blocks = []
            for kb in range(r + 2):
                key = keys[p] if kb == 0 else qkv[kb * 128 - 128 : kb * 128, COLS + p * 128 : COLS + p * 128 + 128]
                part = lax.dot_general(key, stacked, (((1,), (1,)), ((), ())), preferred_element_type=jnp.float32)
                blocks.append(part + tiles[p, r + 1 - kb])
            top = functools.reduce(jnp.maximum, [jnp.max(b, 0, keepdims=True) for b in blocks])
            probs = [jnp.exp(b - top) for b in blocks]
            denom = functools.reduce(jnp.add, [jnp.sum(b, 0, keepdims=True) for b in probs])
            probs = jnp.concatenate([b.astype(jnp.bfloat16) for b in probs], 0)
            out = jnp.dot(values[p][:, : (r + 2) * 128], probs, preferred_element_type=jnp.float32) / denom
            pair = jnp.concatenate([out[:64, :128], out[64:, 128:]], 0)
            asend[r, :, lanes] = pair.T.astype(jnp.bfloat16)

    def attn_copy(r):
        return remote(asend.at[r], aall.at[group], at_s.at[r], at_r.at[group], at(zh, side, r))

    own_attn = pltpu.make_async_copy(asend.at[t], aall.at[group], loc.at[6])

    for r in (3, 0, 2, 1):
        attend(r)
        stays = leader & (t == r)

        @pl.when(stays)
        def _():
            own_attn.start()

        @pl.when(jnp.logical_not(stays))
        def _():
            attn_copy(r).start()

        if r == 0:
            each(o_tracks, "second", 1)

    each(o_tracks, "complete", 1)
    for hh in range(2):
        core_out(hh, c).start()
    load_wo.wait()
    for hh in range(2):
        core_out(hh, 1 - c).wait_recv()

    def attn_arrived(g):
        remote(asend.at[0], aall.at[g], at_s.at[0], at_r.at[g], core).wait_recv()

    total = None
    for rho in range(-1, 3):
        g = lax.rem(t + 1 + rho, 4)
        if rho < 0:
            @pl.when(leader)
            def _():
                own_attn.wait()

            @pl.when(jnp.logical_not(leader))
            def _():
                attn_arrived(g)
        else:
            attn_arrived(g)
        weights = won[...] if rho < 0 else wo[rho]
        part = jnp.dot(aall[g], weights, preferred_element_type=jnp.float32)
        total = part if total is None else total + part
    length = length_ref[request_ref[s]]
    position = t * ROWS + lax.broadcasted_iota(jnp.int32, (ROWS, D), 0)
    out_ref[...] = jnp.where(position < length, total, 0.0).astype(jnp.bfloat16)

    for kv in range(2):
        for k, reader in enumerate(readers):
            prefix_copy(k, kv, zh, c, reader).wait_send()

        @pl.when(jnp.logical_not(leader))
        def _():
            prefix_copy(3, kv, zh, c, core).wait_send()

    send_table.wait_send()
    for hh in range(2):
        weight_piece(hh).wait_send()
        core_out(hh, c).wait_send()
        for d in range(1, 4):
            out_piece(d, hh).wait_send()
    for j in range(CH):
        own_copy(j).wait_send()

    @pl.when(leader)
    def _():
        for j in range(CH):
            for k in range(4):
                sibling_copy(k, j).wait_send()
        for hh in range(2):
            for i in range(4):
                core_weights(hh, i, c).wait_send()

    @pl.when(leader & inner)
    def _():
        for j in range(CH):
            for k in range(2, 4):
                forward_copy(k, j).wait_send()

    for track in (*w_tracks, *p_tracks, *o_tracks):
        track.drain()
    for r in range(TP):
        @pl.when(jnp.logical_not(leader & (t == r)))
        def _():
            attn_copy(r).wait_send()


def body(
    hidden,
    norm_gain,
    qkv_weight,
    out_weight,
    bias_table,
    prefix_cache,
    suffix_lengths,
    request_of_slot,
    block_of_slot,
    bias_bucket,
):
    vmem, smem = pl.BlockSpec(memory_space=pltpu.VMEM), pl.BlockSpec(memory_space=pltpu.SMEM)
    hbm = pl.BlockSpec(memory_space=pltpu.HBM)
    dma = pltpu.SemaphoreType.DMA
    bf16, f32 = jnp.bfloat16, jnp.float32
    out = pl.pallas_call(
        kernel,
        name="sublayer",
        out_shape=jax.ShapeDtypeStruct((ROWS, D), bf16),
        in_specs=[smem, smem, smem, hbm, vmem, hbm, hbm, hbm, vmem, vmem],
        out_specs=vmem,
        scratch_shapes=[
            pltpu.VMEM((2, 3, D, COLS), bf16),
            pltpu.VMEM((SLOT, D), bf16),
            pltpu.VMEM((SLOT, D), bf16),
            pltpu.VMEM((SLOT, 3 * COLS), f32),
            pltpu.VMEM((SLOT, 3 * COLS), bf16),
            pltpu.VMEM((PB, 2, COLS), bf16),
            pltpu.VMEM((2, PB, COLS), bf16),
            pltpu.VMEM((2, CACHE, COLS), bf16),
            pltpu.VMEM((HEADS, BUCKETS), f32),
            pltpu.VMEM((HEADS, PREFIX + DIST), f32),
            pltpu.VMEM((HEADS // 2, 5, 128, 256), f32),
            pltpu.VMEM((3, COLS, D), bf16),
            pltpu.VMEM((COLS, D), bf16),
            pltpu.VMEM((TP, ROWS, COLS), bf16),
            pltpu.VMEM((TP, ROWS, COLS), bf16),
            dma((7,)), dma((CH,)), dma((4, CH)), dma((4, CH)), dma((4, CH)),
            dma((2,)), dma((2,)), dma((1,)), dma((1,)), dma((4, 2)), dma((4, 2)), dma((3, 2)), dma((3, 2)),
            dma((2, 2, 4)), dma((2, 2, 4)), dma((2, 2, 4)), dma((2, 2, 4)), dma((2, 2, 4)), dma((2, 2, 4)),
            dma((2, 4)), dma((2, 4)), dma((2,)), dma((2,)), dma((4,)), dma((4,)),
        ],
        compiler_params=pltpu.CompilerParams(collective_id=0, has_side_effects=True, vmem_limit_bytes=60 << 20),
    )(
        request_of_slot,
        block_of_slot,
        suffix_lengths,
        hidden[0],
        norm_gain.reshape(D // 128, 128),
        qkv_weight.transpose(1, 0, 2),
        prefix_cache,
        out_weight,
        bias_bucket.reshape(DIST // 128, 128),
        bias_table.T,
    )
    return out[None]


def solution(mesh):
    return jax.shard_map(
        body,
        mesh=mesh,
        in_specs=(
            P("seq", "tp", None),
            P(),
            P(None, None, "tp"),
            P("tp", None),
            P(None, "tp"),
            P("seq", None, "tp"),
            P(),
            P(),
            P(),
            P(),
        ),
        out_specs=P("seq", "tp", None),
        check_vma=False,
    )
```

time: 1290 us -> 99.7 us (0.08)
  local copies, waits for them, and re-layouts: 1190 us -> 1.88 us
  Pallas kernels: 0 us -> 97.6 us
  waiting for transfers between devices: 53.6 us -> 0 us
  matrix products: 18.4 us -> 0 us
  between operations: 17.3 us -> 0.01 us
    gather x5 -> x0, local copies, waits for them, and re-layouts: 1170 us -> none  [the longest x4 1170 us: attend(): jnp.take(bias_t, jnp.clip(distance, 0, dist_count - 1), axis=1)]
    pallas_call x0 -> x1, Pallas kernels: none -> 97.6 us  [body(): pl.pallas_call(kernel, name='sublayer', out_shape=jax.ShapeDtypeStruct((R...]
    reduce_scatter x1 -> x0, waiting for transfers between devices: 52.9 us -> none  [body(): lax.psum_scatter(jnp.where(alive[:, None], product, 0.0).astype(jnp.bfloa...]
    dot_general x7 -> x0, matrix products: 18.4 us -> none  [the longest x1 6.89 us: body(): jnp.dot(normed, weights, preferred_element_type=jnp.float32)]
  transfers between devices with their start and end apart: 3 -> 0, of which waited for: 1 -> 0; matrix products, arithmetic and copies ran while one was open for 92% -> 0% of each run, Pallas kernels for 0% -> 0%
where the time goes in v2:
time: 99.7 us; the launch traced here: 99.5 us
  Pallas kernels  97.6 us (98%)
  local copies, waits for them, and re-layouts  1.88 us (2%)
    pallas_call x1, Pallas kernels, body(): pl.pallas_call(kernel, name='sublayer', out_shape=jax.ShapeDtypeStruct((R...  97.6 us

profile of v2, /device:TPU:1, one launch (start us, length us, event | category | flops | bytes accessed | tf_op | source)
XLA Modules:
  0.0 99.5 jit_solution(13117052717023804418)
XLA Ops:
  0.0 97.6 %sublayer.1 = bf16[128,2048]{1,0:T(8,128)(2,1)} custom-call(s32[64]{0:T(128)} %request_ref.1, s32[64]{0:T(128)} %block_ref.1, s32[64]{0:T(128)} %length_ref.1, bf16[128,2048]{1,0:T(8,128)(2,1)} %bitcast.8, bf16[16,128]{1,0:T(8,128)(2,1)} %bitcast.9, bf16[3,2048,512]{2,1,0:T(8,128)(2,1)} %bitcast.6, bf16[8,2,512]{2,1,0:T(2,128)(2,1)} %pref.1, ...), custom_call_target="tpu_custom_call" | custom-call | tf_op jit(solution)/shard_map/sublayer/pallas_call | solution.py:522
  97.7 1.9 %copy.12 = bf16[1,128,2048]{2,1,0:T(8,128)(2,1)} copy(bf16[1,128,2048]{2,1,0:T(8,128)(2,1)} %bitcast.7) | data formatting | bytes 1048576

commit v3 on v2

--- a/solution.py
+++ b/solution.py
@@ -36,53 +36,64 @@
 
 
 class Track:
-    def __init__(self, view, columns, off, unit, me, peers, send, recv):
-        self.view, self.columns, self.off, self.unit = view, columns, off, unit
+    def __init__(self, view, columns, off, unit, step, me, peers, send, recv):
+        self.view, self.columns, self.off, self.unit, self.step = view, columns, off, unit, step
         self.me, self.peers, self.send, self.recv = me, peers, send, recv
 
     def region(self, stage, i, part=None):
         count = self.unit if stage == 0 else 4 * self.unit
-        start = self.off + (self.me[1] * 4 * self.unit + i * self.unit if stage == 0 else i * 4 * self.unit)
+        start = self.off + (self.me[1] * self.step + i * self.unit if stage == 0 else i * self.step)
         half = self.columns // 2
         columns = pl.ds(0, self.columns) if part is None else pl.ds(part * half, half)
         return self.view(pl.ds(aligned(start, self.unit), count), columns)
 
-    def copy(self, stage, k, i):
-        region = self.region(stage, i, None if k < 2 else k - 2)
-        return remote(region, region, self.send.at[stage, k], self.recv.at[stage, k], self.peers[stage][k % 2])
-
-    def near(self, stage):
+    def near(self, stage, k, part, i):
+        region = self.region(stage, i, part)
+        index = k * 2 + part
+        return remote(region, region, self.send.at[stage, index], self.recv.at[stage, index], self.peers[stage][k])
+
+    def far(self, stage, k, i):
+        region = self.region(stage, i, k)
+        return remote(region, region, self.send.at[stage, 4 + k], self.recv.at[stage, 4 + k], self.peers[stage][k])
+
+    def around(self, stage):
         me = self.me[stage]
         return lax.rem(me + 3, 4), lax.rem(me + 1, 4), lax.rem(me + 2, 4)
 
     def first(self, stage):
+        for k, part in ((0, 0), (1, 1), (0, 1), (1, 0)):
+            self.near(stage, k, part, self.me[stage]).start()
+
+    def second(self, stage):
+        behind, ahead, _ = self.around(stage)
+        for k, i in enumerate((behind, ahead)):
+            self.near(stage, k, k, i).wait_recv()
+            self.far(stage, k, i).start()
+
+    def rest(self, stage):
+        behind, ahead, _ = self.around(stage)
+        for k, i in enumerate((behind, ahead)):
+            self.near(stage, k, 1 - k, i).wait_recv()
+
+    def complete(self, stage):
+        opposite = self.around(stage)[2]
         for k in range(2):
-            self.copy(stage, k, self.me[stage]).start()
-
-    def second(self, stage):
-        behind, ahead, _ = self.near(stage)
-        self.copy(stage, 0, behind).wait_recv()
-        self.copy(stage, 1, ahead).wait_recv()
-        self.copy(stage, 2, behind).start()
-        self.copy(stage, 3, ahead).start()
-
-    def complete(self, stage):
-        far = self.near(stage)[2]
-        self.copy(stage, 2, far).wait_recv()
-        self.copy(stage, 3, far).wait_recv()
-
-    def drain(self):
-        for stage in range(2):
-            behind, ahead, _ = self.near(stage)
-            for k, i in enumerate((self.me[stage], self.me[stage], behind, ahead)):
-                self.copy(stage, k, i).wait_send()
+            self.far(stage, k, opposite).wait_recv()
+
+    def drain(self, stages=(0, 1)):
+        for stage in stages:
+            behind, ahead, _ = self.around(stage)
+            for k, i in enumerate((behind, ahead)):
+                for part in range(2):
+                    self.near(stage, k, part, self.me[stage]).wait_send()
+                self.far(stage, k, i).wait_send()
 
 
 def kernel(
     request_ref, block_ref, length_ref, hid, gain_ref, w_hbm, pref, wo_hbm, bucket_ref, table_ref, out_ref,
     wbuf, hbuf, nbuf, acc, qkv, prefv, kvown, pbuf, tab, bias, tiles, wo, won, asend, aall,
     loc, own_s, sib_s, fwd_s, h_r, wz_s, wz_r, tb_s, tb_r, pz_s, pz_r, oz_s, oz_r,
-    wt_s, wt_r, pt_s, pt_r, ot_s, ot_r, wc_s, wc_r, oc_s, oc_r, at_s, at_r,
+    wt_s, wt_r, pt_s, pt_r, ot_s, ot_r, wn_s, wn_r, wf_s, wf_r, wb_s, wb_r, oc_s, oc_r, at_s, at_r,
 ):
     s = lax.axis_index("seq")
     t = lax.axis_index("tp")
@@ -97,20 +108,27 @@
     def at(zh_, c_, t_):
         return (((x * 4 + y) * 2 + zh_) * 2 + c_, t_)
 
-    def column(x_, y_):
-        return (((x_ * 4 + y_) * 2 + zh) * 2 + c, t)
+    def column(x_, y_, c_):
+        return (((x_ * 4 + y_) * 2 + zh) * 2 + c_, t)
 
     def along(step):
         other = lax.rem(zh * 4 + t + step + 8, 8)
         return at(other // 4, c, lax.rem(other, 4))
 
-    xs = (column(lax.rem(x + 1, 4), y), column(lax.rem(x + 3, 4), y))
-    ys = (column(x, lax.rem(y + 1, 4)), column(x, lax.rem(y + 3, 4)))
+    x1, x3, y1, y3 = lax.rem(x + 1, 4), lax.rem(x + 3, 4), lax.rem(y + 1, 4), lax.rem(y + 3, 4)
+    foreign = 1 - side
+    xs, xf = [(column(x1, y, c_), column(x3, y, c_)) for c_ in (c, foreign)]
+    ys, yf = [(column(x, y1, c_), column(x, y3, c_)) for c_ in (c, foreign)]
     core = at(zh, 1 - c, t)
 
     partners = [at(zh, lax.rem(c + dc, 2), lax.rem(t + dt, 4)) for dt in range(4) for dc in range(2) if dt or dc]
     partners += [at(1 - zh, c_, t_) for t_ in (t, across) for c_ in (c, 1 - c)]
-    partners += [*xs, *ys]
+    partners += [at(1 - zh, c, 3 - t)]
+    partners += [
+        (((x_ * 4 + y_) * 2 + zh) * 2 + c_, t)
+        for x_, y_ in ((x1, y), (x3, y), (x, y1), (x, y3))
+        for c_ in (c, 1 - c)
+    ]
     barrier = pltpu.get_barrier_semaphore()
     for partner in partners:
         pl.semaphore_signal(barrier, inc=1, device_id=partner, device_id_type=MESH)
@@ -133,6 +151,15 @@
     kvown[1] = both[:, 1, :].astype(jnp.bfloat16)
     pl.semaphore_wait(barrier, len(partners))
 
+    def weight_row(hh):
+        return hh * 1024 + c * 128 + ((y * 256 + x * 32) if hh == 0 else (x * 256 + y * 32))
+
+    def weight_piece(hh):
+        rows = pl.ds(aligned(weight_row(hh), 32), 32)
+        return remote(
+            w_hbm.at[:, rows], wbuf.at[1, :, rows], wz_s.at[hh], wz_r.at[hh], along(2 if hh == 0 else -2)
+        )
+
     def prefix_row(kv, zh_, c_):
         place = (y * 4 + x) if kv == 0 else (x * 4 + y)
         return pl.ds(aligned((place * 4 + zh_ * 2 + c_) * PB, PB), PB)
@@ -159,16 +186,6 @@
 
     send_table = remote(table_ref, tab, tb_s.at[0], tb_r.at[0], at(zh, c, across))
     send_table.start()
-
-    def weight_row(hh):
-        return hh * 1024 + c * 512 + ((y * 4 + x) if hh == 0 else (x * 4 + y)) * 32
-
-    def weight_piece(hh):
-        rows = pl.ds(aligned(weight_row(hh), 32), 32)
-        return remote(
-            w_hbm.at[:, rows], wbuf.at[1, :, rows], wz_s.at[hh], wz_r.at[hh], along(2 if hh == 0 else -2)
-        )
-
     for hh in range(2):
         weight_piece(hh).start()
 
@@ -195,9 +212,6 @@
         return remote(chunk(q, j), chunk(q, j), fwd_s.at[k, j], h_r.at[q, j], at(zh, c, beside))
 
     for j in range(CH):
-        own_copy(j).start()
-
-    for j in range(CH):
         @pl.when(leader)
         def _():
             sibling_copy(0, j).start()
@@ -207,9 +221,8 @@
 
     def out_piece(d, hh):
         rows = pl.ds(aligned(out_row(hh), 8), 8)
-        return remote(
-            wo_hbm.at[rows], wo.at[3 - d, rows], oz_s.at[d - 1, hh], oz_r.at[3 - d, hh], at(zh, c, lax.rem(t + d, 4))
-        )
+        step = (1, (2, -2)[hh], -1)[d - 1]
+        return remote(wo_hbm.at[rows], wo.at[3 - d, rows], oz_s.at[d - 1, hh], oz_r.at[3 - d, hh], along(step))
 
     def arrive(k, j):
         if k == 0:
@@ -228,28 +241,78 @@
                 def _():
                     forward_copy(k, j).start()
 
-    def tracks(views, columns, offs, unit, send, recv):
-        first = Track(views[0], columns, offs[0], unit, (x, y), (xs, ys), send.at[0], recv.at[0])
-        other = Track(views[1], columns, offs[1], unit, (y, x), (ys, xs), send.at[1], recv.at[1])
+    def tracks(views, columns, offs, unit, step, send, recv):
+        first = Track(views[0], columns, offs[0], unit, step, (x, y), (xs, ys), send.at[0], recv.at[0])
+        other = Track(views[1], columns, offs[1], unit, step, (y, x), (ys, xs), send.at[1], recv.at[1])
         return first, other
 
     w_view = lambda rows, columns: wbuf.at[1, :, rows, columns]
     o_view = lambda rows, columns: wo.at[:, rows, columns]
-    w_tracks = tracks((w_view, w_view), COLS, (c * 512, 1024 + c * 512), 32, wt_s, wt_r)
+    w_tracks = tracks((w_view, w_view), COLS, (c * 128, 1024 + c * 128), 32, 256, wt_s, wt_r)
     p_tracks = tracks(
         (lambda rows, columns: pbuf.at[0, rows, columns], lambda rows, columns: pbuf.at[1, rows, columns]),
-        COLS, (0, 0), 32, pt_s, pt_r,
+        COLS, (0, 0), 32, 128, pt_s, pt_r,
     )
-    o_tracks = tracks((o_view, o_view), D, (c * 128, 256 + c * 128), 8, ot_s, ot_r)
-
-    def core_weights(hh, i, core_):
-        start = hh * 1024 + core_ * 512 + i * 128
-        region = wbuf.at[1, :, pl.ds(aligned(start, 128), 128)]
-        return remote(region, region, wc_s.at[hh, i], wc_r.at[hh, i], core)
-
-    def core_out(hh, core_):
-        region = wo.at[:, pl.ds(aligned(hh * 256 + core_ * 128, 128), 128)]
-        return remote(region, region, oc_s.at[hh], oc_r.at[hh], core)
+    o_tracks = tracks((o_view, o_view), D, (c * 128, 256 + c * 128), 8, 32, ot_s, ot_r)
+
+    places = ((y, y3, y1, yf), (x, x3, x1, xf))
+
+    def w_region(hh, core_, i, part=None):
+        rows = pl.ds(aligned(hh * 1024 + i * 256 + core_ * 128, 128), 128)
+        half = COLS // 2
+        return wbuf.at[1, :, rows, pl.ds(0, COLS) if part is None else pl.ds(part * half, half)]
+
+    def w_near(hh, k, part, core_, i):
+        region = w_region(hh, core_, i, part)
+        return remote(region, region, wn_s.at[hh, k, part], wn_r.at[hh, core_, k, part], places[hh][3][k])
+
+    def w_far(hh, k, core_, i):
+        region = w_region(hh, core_, i, k)
+        return remote(region, region, wf_s.at[hh, core_, k], wf_r.at[hh, core_, k], places[hh][3][k])
+
+    def w_beside(hh, core_):
+        region = w_region(hh, core_, places[hh][0])
+        return remote(region, region, wb_s.at[hh], wb_r.at[hh], core)
+
+    def w_first():
+        for k, part in ((0, 0), (1, 1), (0, 1), (1, 0)):
+            for hh in range(2):
+                w_near(hh, k, part, c, places[hh][0]).start()
+
+        @pl.when(leader)
+        def _():
+            for hh in range(2):
+                w_beside(hh, c).start()
+
+    def w_second():
+        @pl.when(jnp.logical_not(leader))
+        def _():
+            for k in range(2):
+                for hh in range(2):
+                    for core_ in range(2):
+                        w_near(hh, k, k, core_, places[hh][1 + k]).wait_recv()
+                        w_far(hh, k, core_, places[hh][1 + k]).start()
+
+    def w_rest():
+        @pl.when(jnp.logical_not(leader))
+        def _():
+            for hh in range(2):
+                w_beside(hh, 1 - c).wait_recv()
+                for k in range(2):
+                    for core_ in range(2):
+                        w_near(hh, k, 1 - k, core_, places[hh][1 + k]).wait_recv()
+
+    def w_complete():
+        @pl.when(jnp.logical_not(leader))
+        def _():
+            for hh in range(2):
+                for k in range(2):
+                    for core_ in range(2):
+                        w_far(hh, k, core_, lax.rem(places[hh][0] + 2, 4)).wait_recv()
+
+    def core_out(hh, core_, i):
+        region = wo.at[:, pl.ds(aligned(hh * 256 + core_ * 128 + i * 32, 32), 32)]
+        return remote(region, region, oc_s.at[hh, i], oc_r.at[hh, i], core)
 
     def each(which, action, stage):
         for track in which:
@@ -262,49 +325,15 @@
         scale = lax.rsqrt(jnp.mean(states * states, -1, keepdims=True) + 1e-06)
         nbuf[rows, :] = (states * scale * gain).astype(jnp.bfloat16)
 
-    for kv in range(2):
-        for zh_ in range(2):
-            for c_ in range(2):
-                mine = leader & (zh == zh_) & (c == c_)
-
-                @pl.when(jnp.logical_not(mine))
-                def _():
-                    prefix_copy(0, kv, zh_, c_, core).wait_recv()
-
-        @pl.when(leader)
-        def _():
-            own_prefix[kv].wait()
-
-    each(p_tracks, "first", 0)
-    send_table.wait_recv()
-
-    for j in range(2):
-        arrive(0, j)
-        arrive(1, j)
-    for hh in range(2):
-        weight_piece(hh).wait_recv()
-    each(w_tracks, "first", 0)
-    each(p_tracks, "second", 0)
-    for d in range(1, 4):
-        for hh in range(2):
-            out_piece(d, hh).start()
-    each(w_tracks, "second", 0)
-    for j in range(2, CH):
-        arrive(0, j)
-        arrive(1, j)
-    each(w_tracks, "complete", 0)
-    each(w_tracks, "first", 1)
-    each(p_tracks, "complete", 0)
-    each(p_tracks, "first", 1)
-
-    bucket = jnp.concatenate([bucket_ref[i : i + 1, :] for i in range(DIST // 128)], 1)
-    bucket = jnp.broadcast_to(bucket, (HEADS, DIST))
-    table = jnp.where(leader, table_ref[...], tab[...])
-    row = jnp.zeros((HEADS, DIST), jnp.float32)
-    for b in range(BUCKETS):
-        row = jnp.where(bucket == b, table[:, b : b + 1], row)
-    bias[:, :PREFIX] = jnp.full((HEADS, PREFIX), NEG, jnp.float32)
-    bias[:, PREFIX:] = row
+    def build_bias():
+        bucket = jnp.concatenate([bucket_ref[i : i + 1, :] for i in range(DIST // 128)], 1)
+        bucket = jnp.broadcast_to(bucket, (HEADS, DIST))
+        table = jnp.where(leader, table_ref[...], tab[...])
+        row = jnp.zeros((HEADS, DIST), jnp.float32)
+        for b in range(BUCKETS):
+            row = jnp.where(bucket == b, table[:, b : b + 1], row)
+        bias[:, :PREFIX] = jnp.full((HEADS, PREFIX), NEG, jnp.float32)
+        bias[:, PREFIX:] = row
 
     def build(h):
         for delta in range(5):
@@ -312,64 +341,96 @@
             rolled = pltpu.roll(window, 0, 1, stride=1, stride_axis=0)
             tiles[h // 2, delta, :, (h % 2) * 128 : (h % 2) * 128 + 128] = rolled[:, 128:]
 
+    def prefix_arrived():
+        for kv in range(2):
+            for zh_ in range(2):
+                for c_ in range(2):
+                    mine = leader & (zh == zh_) & (c == c_)
+
+                    @pl.when(jnp.logical_not(mine))
+                    def _():
+                        prefix_copy(0, kv, zh_, c_, core).wait_recv()
+
+            @pl.when(leader)
+            def _():
+                own_prefix[kv].wait()
+
+    prefix_arrived()
+    each(p_tracks, "first", 0)
+    send_table.wait_recv()
+    build_bias()
+    for hh in range(2):
+        weight_piece(hh).wait_recv()
+    each(w_tracks, "first", 0)
     for j in range(CH):
+        own_copy(j).start()
+    for d in range(1, 4):
+        for hh in range(2):
+            out_piece(d, hh).start()
+    each(p_tracks, "second", 0)
+    each(p_tracks, "rest", 0)
+    each(p_tracks, "complete", 0)
+    each(p_tracks, "first", 1)
+    for h in range(3):
+        build(h)
+    each(w_tracks, "second", 0)
+    each(w_tracks, "rest", 0)
+    for j in range(CH):
+        arrive(0, j)
+    each(p_tracks, "second", 1)
+    arrive(1, 0)
+    arrive(2, 0)
+    each(w_tracks, "complete", 0)
+    w_first()
+    for j in range(1, CH):
+        arrive(1, j)
         arrive(2, j)
-        build(j)
-    each(p_tracks, "second", 1)
+
+    @pl.when(leader)
+    def _():
+        load_own.wait()
+
+    norm(0)
+    for j in range(CH):
+        arrive(3, j)
+    w_second()
     for rho in range(3):
         for hh in range(2):
             out_piece(3 - rho, hh).wait_recv()
     each(o_tracks, "first", 0)
-
-    @pl.when(leader)
-    def _():
-        load_own.wait()
-
-    norm(0)
+    norm(1)
+    for h in range(3, HEADS):
+        build(h)
+    each(p_tracks, "rest", 1)
+    each(p_tracks, "complete", 1)
     each(o_tracks, "second", 0)
-    for j in range(CH):
-        arrive(3, j)
-        build(CH + j)
-    norm(1)
-    each(w_tracks, "second", 1)
-    each(o_tracks, "complete", 0)
-
-    @pl.when(leader)
-    def _():
-        for hh, me in ((0, y), (1, x)):
-            for i in (me, lax.rem(me + 1, 4), lax.rem(me + 3, 4)):
-                core_weights(hh, i, c).start()
-
     norm(2)
     norm(3)
-    each(p_tracks, "complete", 1)
-    each(w_tracks, "complete", 1)
-    each(o_tracks, "first", 1)
-
-    @pl.when(leader)
-    def _():
-        for hh, me in ((0, y), (1, x)):
-            core_weights(hh, lax.rem(me + 2, 4), c).start()
-
+    w_rest()
     load_w.wait()
     which = jnp.where(leader, 0, 1)
-    for step, (hh, core_) in enumerate(((0, c), (1, c), (0, 1 - c), (1, 1 - c))):
-        if step >= 2:
-            @pl.when(jnp.logical_not(leader))
-            def _():
-                for i in range(4):
-                    core_weights(hh, i, core_).wait_recv()
-
-        rows = pl.ds(aligned(hh * 1024 + core_ * 512, 512), 512)
-        for i in range(3):
-            columns = slice(i * COLS, (i + 1) * COLS)
+
+    def product(i, slices):
+        total = None
+        for hh, place in slices:
+            rows = pl.ds(aligned(hh * 1024 + place * 256, 256), 256)
             part = jnp.dot(nbuf[:, rows], wbuf[which, i, rows, :], preferred_element_type=jnp.float32)
-            if step == 0:
-                acc[:, columns] = part
-            elif step < 3:
-                acc[:, columns] += part
-            else:
-                qkv[:, columns] = (acc[:, columns] + part).astype(jnp.bfloat16)
+            total = part if total is None else total + part
+        return total
+
+    for i in range(3):
+        acc[:, i * COLS : (i + 1) * COLS] = product(i, [(hh, places[hh][k]) for hh in range(2) for k in range(3)])
+        if i == 0:
+            each(o_tracks, "rest", 0)
+            each(o_tracks, "complete", 0)
+            each(o_tracks, "first", 1)
+            for hh in range(2):
+                core_out(hh, c, places[hh][0]).start()
+    w_complete()
+    for i in range(3):
+        columns = slice(i * COLS, (i + 1) * COLS)
+        far = product(i, [(hh, lax.rem(places[hh][0] + 2, 4)) for hh in range(2)])
+        qkv[:, columns] = (acc[:, columns] + far).astype(jnp.bfloat16)
 
     slot = ((x * 4 + y) * 2 + zh) * 2 + side
     first_row = request_ref[slot] // RG * PREFIX
@@ -430,15 +491,21 @@
         def _():
             attn_copy(r).start()
 
-        if r == 0:
+        if r == 3:
             each(o_tracks, "second", 1)
+        if r == 2:
+            each(o_tracks, "rest", 1)
+            for hh in range(2):
+                for k in range(2):
+                    core_out(hh, c, places[hh][1 + k]).start()
 
     each(o_tracks, "complete", 1)
     for hh in range(2):
-        core_out(hh, c).start()
+        core_out(hh, c, lax.rem(places[hh][0] + 2, 4)).start()
     load_wo.wait()
     for hh in range(2):
-        core_out(hh, 1 - c).wait_recv()
+        for i in range(4):
+            core_out(hh, 1 - c, i).wait_recv()
 
     def attn_arrived(g):
         remote(asend.at[0], aall.at[g], at_s.at[0], at_r.at[g], core).wait_recv()
@@ -474,9 +541,13 @@
     send_table.wait_send()
     for hh in range(2):
         weight_piece(hh).wait_send()
-        core_out(hh, c).wait_send()
+        for i in range(4):
+            core_out(hh, c, i).wait_send()
         for d in range(1, 4):
             out_piece(d, hh).wait_send()
+        for k in range(2):
+            for part in range(2):
+                w_near(hh, k, part, c, places[hh][0]).wait_send()
     for j in range(CH):
         own_copy(j).wait_send()
 
@@ -486,8 +557,14 @@
             for k in range(4):
                 sibling_copy(k, j).wait_send()
         for hh in range(2):
-            for i in range(4):
-                core_weights(hh, i, c).wait_send()
+            w_beside(hh, c).wait_send()
+
+    @pl.when(jnp.logical_not(leader))
+    def _():
+        for hh in range(2):
+            for k in range(2):
+                for core_ in range(2):
+                    w_far(hh, k, core_, places[hh][1 + k]).wait_send()
 
     @pl.when(leader & inner)
     def _():
@@ -495,7 +572,9 @@
             for k in range(2, 4):
                 forward_copy(k, j).wait_send()
 
-    for track in (*w_tracks, *p_tracks, *o_tracks):
+    for track in w_tracks:
+        track.drain((0,))
+    for track in (*p_tracks, *o_tracks):
         track.drain()
     for r in range(TP):
         @pl.when(jnp.logical_not(leader & (t == r)))
@@ -543,8 +622,9 @@
             pltpu.VMEM((TP, ROWS, COLS), bf16),
             dma((7,)), dma((CH,)), dma((4, CH)), dma((4, CH)), dma((4, CH)),
             dma((2,)), dma((2,)), dma((1,)), dma((1,)), dma((4, 2)), dma((4, 2)), dma((3, 2)), dma((3, 2)),
-            dma((2, 2, 4)), dma((2, 2, 4)), dma((2, 2, 4)), dma((2, 2, 4)), dma((2, 2, 4)), dma((2, 2, 4)),
-            dma((2, 4)), dma((2, 4)), dma((2,)), dma((2,)), dma((4,)), dma((4,)),
+            dma((2, 2, 6)), dma((2, 2, 6)), dma((2, 2, 6)), dma((2, 2, 6)), dma((2, 2, 6)), dma((2, 2, 6)),
+            dma((2, 2, 2)), dma((2, 2, 2, 2)), dma((2, 2, 2)), dma((2, 2, 2)), dma((2,)), dma((2,)),
+            dma((2, 4)), dma((2, 4)), dma((4,)), dma((4,)),
         ],
         compiler_params=pltpu.CompilerParams(collective_id=0, has_side_effects=True, vmem_limit_bytes=60 << 20),
     )(

time: 99.7 us -> 76.1 us (0.76)
  Pallas kernels: 97.6 us -> 73.9 us
    pallas_call x1, Pallas kernels: 97.6 us -> 73.9 us  [body(): pl.pallas_call(kernel, name='sublayer', out_shape=jax.ShapeDtypeStruct((R...]
where the time goes in v3:
time: 76.1 us; the launch traced here: 75.8 us
  Pallas kernels  73.9 us (97%)
  local copies, waits for them, and re-layouts  1.88 us (2%)
    pallas_call x1, Pallas kernels, body(): pl.pallas_call(kernel, name='sublayer', out_shape=jax.ShapeDtypeStruct((R...  73.9 us
    unnamed x1, local copies, waits for them, and re-layouts  1.88 us

profile of v3, /device:TPU:1, one launch (start us, length us, event | category | flops | bytes accessed | tf_op | source)
XLA Modules:
  0.0 75.8 jit_solution(12674487882429426359)
XLA Ops:
  0.0 73.9 %sublayer.1 = bf16[128,2048]{1,0:T(8,128)(2,1)} custom-call(s32[64]{0:T(128)} %request_ref.1, s32[64]{0:T(128)} %block_ref.1, s32[64]{0:T(128)} %length_ref.1, bf16[128,2048]{1,0:T(8,128)(2,1)} %bitcast.8, bf16[16,128]{1,0:T(8,128)(2,1)} %bitcast.9, bf16[3,2048,512]{2,1,0:T(8,128)(2,1)} %bitcast.6, bf16[8,2,512]{2,1,0:T(2,128)(2,1)} %pref.1, ...), custom_call_target="tpu_custom_call" | custom-call | tf_op jit(solution)/shard_map/sublayer/pallas_call | solution.py:601
  73.9 1.9 %copy.12 = bf16[1,128,2048]{2,1,0:T(8,128)(2,1)} copy(bf16[1,128,2048]{2,1,0:T(8,128)(2,1)} %bitcast.7) | data formatting | bytes 1048576

commit v4 on v3

--- a/solution.py
+++ b/solution.py
@@ -202,6 +202,9 @@
     def own_copy(j):
         return remote(hid.at[pl.ds(j * CROWS, CROWS)], chunk(t, j), own_s.at[j], h_r.at[t, j], own_to)
 
+    for j in range(1):
+        own_copy(j).start()
+
     def sibling_copy(k, j):
         q = quarter(k)
         src = hid.at[pl.ds(j * CROWS, CROWS)] if k == 0 else chunk(q, j)
@@ -225,21 +228,21 @@
         return remote(wo_hbm.at[rows], wo.at[3 - d, rows], oz_s.at[d - 1, hh], oz_r.at[3 - d, hh], along(step))
 
     def arrive(k, j):
-        if k == 0:
-            @pl.when(jnp.logical_not(leader))
+        @pl.when(leader)
+        def _():
+            sibling_copy(k, j).wait_recv()
+            sibling_copy(k, j).start()
+
+        if k >= 2:
+            @pl.when(leader & inner)
             def _():
-                sibling_copy(0, j).wait_recv()
-        else:
-            sibling_copy(k, j).wait_recv()
-
-            @pl.when(leader)
-            def _():
-                sibling_copy(k, j).start()
-
-            if k >= 2:
-                @pl.when(leader & inner)
-                def _():
-                    forward_copy(k, j).start()
+                forward_copy(k, j).start()
+
+    def arrived(k):
+        @pl.when(jnp.logical_not(leader))
+        def _():
+            for j in range(CH):
+                sibling_copy(k, j).wait_recv()
 
     def tracks(views, columns, offs, unit, step, send, recv):
         first = Track(views[0], columns, offs[0], unit, step, (x, y), (xs, ys), send.at[0], recv.at[0])
@@ -319,6 +322,7 @@
             getattr(track, action)(stage)
 
     def norm(k):
+        arrived(k)
         rows = pl.ds(aligned(quarter(k) * ROWS, ROWS), ROWS)
         gain = jnp.concatenate([gain_ref[i : i + 1, :].astype(jnp.float32) for i in range(D // 128)], 1)
         states = hbuf[rows, :].astype(jnp.float32)
@@ -357,32 +361,30 @@
 
     prefix_arrived()
     each(p_tracks, "first", 0)
-    send_table.wait_recv()
-    build_bias()
     for hh in range(2):
         weight_piece(hh).wait_recv()
     each(w_tracks, "first", 0)
-    for j in range(CH):
+    for j in range(1, CH):
         own_copy(j).start()
     for d in range(1, 4):
         for hh in range(2):
             out_piece(d, hh).start()
     each(p_tracks, "second", 0)
     each(p_tracks, "rest", 0)
+    send_table.wait_recv()
+    build_bias()
+    each(w_tracks, "second", 0)
     each(p_tracks, "complete", 0)
     each(p_tracks, "first", 1)
-    for h in range(3):
-        build(h)
-    each(w_tracks, "second", 0)
     each(w_tracks, "rest", 0)
-    for j in range(CH):
-        arrive(0, j)
-    each(p_tracks, "second", 1)
-    arrive(1, 0)
-    arrive(2, 0)
     each(w_tracks, "complete", 0)
     w_first()
-    for j in range(1, CH):
+    for j in range(2):
+        arrive(1, j)
+        arrive(2, j)
+    build(0)
+    each(p_tracks, "second", 1)
+    for j in range(2, CH):
         arrive(1, j)
         arrive(2, j)
 
@@ -391,21 +393,25 @@
         load_own.wait()
 
     norm(0)
-    for j in range(CH):
-        arrive(3, j)
-    w_second()
     for rho in range(3):
         for hh in range(2):
             out_piece(3 - rho, hh).wait_recv()
     each(o_tracks, "first", 0)
+    w_second()
+    for j in range(CH):
+        arrive(3, j)
+    build(1)
+    build(2)
+    each(o_tracks, "second", 0)
     norm(1)
     for h in range(3, HEADS):
         build(h)
     each(p_tracks, "rest", 1)
     each(p_tracks, "complete", 1)
-    each(o_tracks, "second", 0)
+    each(o_tracks, "rest", 0)
     norm(2)
     norm(3)
+    each(o_tracks, "complete", 0)
     w_rest()
     load_w.wait()
     which = jnp.where(leader, 0, 1)
@@ -421,8 +427,6 @@
     for i in range(3):
         acc[:, i * COLS : (i + 1) * COLS] = product(i, [(hh, places[hh][k]) for hh in range(2) for k in range(3)])
         if i == 0:
-            each(o_tracks, "rest", 0)
-            each(o_tracks, "complete", 0)
             each(o_tracks, "first", 1)
             for hh in range(2):
                 core_out(hh, c, places[hh][0]).start()
@@ -502,6 +506,50 @@
     each(o_tracks, "complete", 1)
     for hh in range(2):
         core_out(hh, c, lax.rem(places[hh][0] + 2, 4)).start()
+    for kv in range(2):
+        for k, reader in enumerate(readers):
+            prefix_copy(k, kv, zh, c, reader).wait_send()
+
+        @pl.when(jnp.logical_not(leader))
+        def _():
+            prefix_copy(3, kv, zh, c, core).wait_send()
+
+    send_table.wait_send()
+    for hh in range(2):
+        weight_piece(hh).wait_send()
+        for d in range(1, 4):
+            out_piece(d, hh).wait_send()
+        for k in range(2):
+            for part in range(2):
+                w_near(hh, k, part, c, places[hh][0]).wait_send()
+    for j in range(CH):
+        own_copy(j).wait_send()
+
+    @pl.when(leader)
+    def _():
+        for j in range(CH):
+            for k in range(4):
+                sibling_copy(k, j).wait_send()
+        for hh in range(2):
+            w_beside(hh, c).wait_send()
+
+    @pl.when(jnp.logical_not(leader))
+    def _():
+        for hh in range(2):
+            for k in range(2):
+                for core_ in range(2):
+                    w_far(hh, k, core_, places[hh][1 + k]).wait_send()
+
+    @pl.when(leader & inner)
+    def _():
+        for j in range(CH):
+            for k in range(2, 4):
+                forward_copy(k, j).wait_send()
+
+    for track in w_tracks:
+        track.drain((0,))
+    for track in (*p_tracks, *o_tracks):
+        track.drain()
     load_wo.wait()
     for hh in range(2):
         for i in range(4):
@@ -529,53 +577,9 @@
     length = length_ref[request_ref[s]]
     position = t * ROWS + lax.broadcasted_iota(jnp.int32, (ROWS, D), 0)
     out_ref[...] = jnp.where(position < length, total, 0.0).astype(jnp.bfloat16)
-
-    for kv in range(2):
-        for k, reader in enumerate(readers):
-            prefix_copy(k, kv, zh, c, reader).wait_send()
-
-        @pl.when(jnp.logical_not(leader))
-        def _():
-            prefix_copy(3, kv, zh, c, core).wait_send()
-
-    send_table.wait_send()
     for hh in range(2):
-        weight_piece(hh).wait_send()
         for i in range(4):
             core_out(hh, c, i).wait_send()
-        for d in range(1, 4):
-            out_piece(d, hh).wait_send()
-        for k in range(2):
-            for part in range(2):
-                w_near(hh, k, part, c, places[hh][0]).wait_send()
-    for j in range(CH):
-        own_copy(j).wait_send()
-
-    @pl.when(leader)
-    def _():
-        for j in range(CH):
-            for k in range(4):
-                sibling_copy(k, j).wait_send()
-        for hh in range(2):
-            w_beside(hh, c).wait_send()
-
-    @pl.when(jnp.logical_not(leader))
-    def _():
-        for hh in range(2):
-            for k in range(2):
-                for core_ in range(2):
-                    w_far(hh, k, core_, places[hh][1 + k]).wait_send()
-
-    @pl.when(leader & inner)
-    def _():
-        for j in range(CH):
-            for k in range(2, 4):
-                forward_copy(k, j).wait_send()
-
-    for track in w_tracks:
-        track.drain((0,))
-    for track in (*p_tracks, *o_tracks):
-        track.drain()
     for r in range(TP):
         @pl.when(jnp.logical_not(leader & (t == r)))
         def _():

time: 76.1 us -> 70.7 us (0.929)
  Pallas kernels: 73.9 us -> 68.6 us
    pallas_call x1, Pallas kernels: 73.9 us -> 68.6 us  [body(): pl.pallas_call(kernel, name='sublayer', out_shape=jax.ShapeDtypeStruct((R...]
where the time goes in v4:
time: 70.7 us; the launch traced here: 70.5 us
  Pallas kernels  68.6 us (97%)
  local copies, waits for them, and re-layouts  1.88 us (3%)
    pallas_call x1, Pallas kernels, body(): pl.pallas_call(kernel, name='sublayer', out_shape=jax.ShapeDtypeStruct((R...  68.6 us
    unnamed x1, local copies, waits for them, and re-layouts  1.88 us

profile of v4, /device:TPU:1, one launch (start us, length us, event | category | flops | bytes accessed | tf_op | source)
XLA Modules:
  0.0 70.5 jit_solution(9491457439631311488)
XLA Ops:
  0.0 68.6 %sublayer.1 = bf16[128,2048]{1,0:T(8,128)(2,1)} custom-call(s32[64]{0:T(128)} %request_ref.1, s32[64]{0:T(128)} %block_ref.1, s32[64]{0:T(128)} %length_ref.1, bf16[128,2048]{1,0:T(8,128)(2,1)} %bitcast.8, bf16[16,128]{1,0:T(8,128)(2,1)} %bitcast.9, bf16[3,2048,512]{2,1,0:T(8,128)(2,1)} %bitcast.6, bf16[8,2,512]{2,1,0:T(2,128)(2,1)} %pref.1, ...), custom_call_target="tpu_custom_call" | custom-call | tf_op jit(solution)/shard_map/sublayer/pallas_call | solution.py:605
  68.6 1.9 %copy.12 = bf16[1,128,2048]{2,1,0:T(8,128)(2,1)} copy(bf16[1,128,2048]{2,1,0:T(8,128)(2,1)} %bitcast.7) | data formatting | bytes 1048576

commit v5 on v4

--- a/solution.py
+++ b/solution.py
@@ -154,10 +154,15 @@
     def weight_row(hh):
         return hh * 1024 + c * 128 + ((y * 256 + x * 32) if hh == 0 else (x * 256 + y * 32))
 
-    def weight_piece(hh):
+    def weight_piece(hh, part):
         rows = pl.ds(aligned(weight_row(hh), 32), 32)
+        columns = pl.ds(part * (COLS // 2), COLS // 2)
         return remote(
-            w_hbm.at[:, rows], wbuf.at[1, :, rows], wz_s.at[hh], wz_r.at[hh], along(2 if hh == 0 else -2)
+            w_hbm.at[:, rows, columns],
+            wbuf.at[1, :, rows, columns],
+            wz_s.at[hh, part],
+            wz_r.at[hh, part],
+            along(2 if hh == 0 else -2),
         )
 
     def prefix_row(kv, zh_, c_):
@@ -186,8 +191,9 @@
 
     send_table = remote(table_ref, tab, tb_s.at[0], tb_r.at[0], at(zh, c, across))
     send_table.start()
-    for hh in range(2):
-        weight_piece(hh).start()
+    for part in range(2):
+        for hh in range(2):
+            weight_piece(hh, part).start()
 
     def quarter(k):
         j = jnp.where(t < 2, 2, 1)
@@ -202,9 +208,6 @@
     def own_copy(j):
         return remote(hid.at[pl.ds(j * CROWS, CROWS)], chunk(t, j), own_s.at[j], h_r.at[t, j], own_to)
 
-    for j in range(1):
-        own_copy(j).start()
-
     def sibling_copy(k, j):
         q = quarter(k)
         src = hid.at[pl.ds(j * CROWS, CROWS)] if k == 0 else chunk(q, j)
@@ -227,15 +230,12 @@
         step = (1, (2, -2)[hh], -1)[d - 1]
         return remote(wo_hbm.at[rows], wo.at[3 - d, rows], oz_s.at[d - 1, hh], oz_r.at[3 - d, hh], along(step))
 
-    def arrive(k, j):
-        @pl.when(leader)
+    def arrive(k, j, ends):
+        @pl.when(leader & (inner != ends))
         def _():
             sibling_copy(k, j).wait_recv()
             sibling_copy(k, j).start()
-
-        if k >= 2:
-            @pl.when(leader & inner)
-            def _():
+            if k >= 2 and not ends:
                 forward_copy(k, j).start()
 
     def arrived(k):
@@ -359,59 +359,66 @@
             def _():
                 own_prefix[kv].wait()
 
-    prefix_arrived()
-    each(p_tracks, "first", 0)
-    for hh in range(2):
-        weight_piece(hh).wait_recv()
-    each(w_tracks, "first", 0)
-    for j in range(1, CH):
-        own_copy(j).start()
     for d in range(1, 4):
         for hh in range(2):
             out_piece(d, hh).start()
+    prefix_arrived()
+    each(p_tracks, "first", 0)
+    for part in range(2):
+        for hh in range(2):
+            weight_piece(hh, part).wait_recv()
+        for k in (part, 1 - part):
+            for track in w_tracks:
+                track.near(0, k, part, track.me[0]).start()
+    for j in range(CH):
+        own_copy(j).start()
     each(p_tracks, "second", 0)
     each(p_tracks, "rest", 0)
     send_table.wait_recv()
     build_bias()
     each(w_tracks, "second", 0)
-    each(p_tracks, "complete", 0)
-    each(p_tracks, "first", 1)
-    each(w_tracks, "rest", 0)
-    each(w_tracks, "complete", 0)
-    w_first()
-    for j in range(2):
-        arrive(1, j)
-        arrive(2, j)
-    build(0)
-    each(p_tracks, "second", 1)
-    for j in range(2, CH):
-        arrive(1, j)
-        arrive(2, j)
-
-    @pl.when(leader)
-    def _():
-        load_own.wait()
-
-    norm(0)
     for rho in range(3):
         for hh in range(2):
             out_piece(3 - rho, hh).wait_recv()
     each(o_tracks, "first", 0)
+    each(p_tracks, "complete", 0)
+    each(p_tracks, "first", 1)
+    for k in range(1, 4):
+        arrive(k, 0, False)
+    each(w_tracks, "rest", 0)
+    each(w_tracks, "complete", 0)
+    w_first()
+    each(o_tracks, "second", 0)
+    for k in range(1, 4):
+        arrive(k, 1, False)
+    each(p_tracks, "second", 1)
+    for j in range(2, CH):
+        for k in range(1, 4):
+            arrive(k, j, False)
+
+    @pl.when(leader)
+    def _():
+        load_own.wait()
+
+    norm(0)
+    for h in range(4):
+        build(h)
+    for j in range(CH):
+        for k in range(1, 4):
+            arrive(k, j, True)
     w_second()
-    for j in range(CH):
-        arrive(3, j)
-    build(1)
-    build(2)
-    each(o_tracks, "second", 0)
+    each(o_tracks, "rest", 0)
+    each(o_tracks, "complete", 0)
+    each(o_tracks, "first", 1)
+    for hh in range(2):
+        core_out(hh, c, places[hh][0]).start()
     norm(1)
-    for h in range(3, HEADS):
+    for h in range(4, HEADS):
         build(h)
     each(p_tracks, "rest", 1)
     each(p_tracks, "complete", 1)
-    each(o_tracks, "rest", 0)
     norm(2)
     norm(3)
-    each(o_tracks, "complete", 0)
     w_rest()
     load_w.wait()
     which = jnp.where(leader, 0, 1)
@@ -426,16 +433,6 @@
 
     for i in range(3):
         acc[:, i * COLS : (i + 1) * COLS] = product(i, [(hh, places[hh][k]) for hh in range(2) for k in range(3)])
-        if i == 0:
-            each(o_tracks, "first", 1)
-            for hh in range(2):
-                core_out(hh, c, places[hh][0]).start()
-    w_complete()
-    for i in range(3):
-        columns = slice(i * COLS, (i + 1) * COLS)
-        far = product(i, [(hh, lax.rem(places[hh][0] + 2, 4)) for hh in range(2)])
-        qkv[:, columns] = (acc[:, columns] + far).astype(jnp.bfloat16)
-
     slot = ((x * 4 + y) * 2 + zh) * 2 + side
     first_row = request_ref[slot] // RG * PREFIX
     lane = lax.broadcasted_iota(jnp.int32, (1, CACHE), 1)
@@ -449,6 +446,12 @@
         match = lax.broadcasted_iota(jnp.int32, (PREFIX, CACHE), 0) == jnp.broadcast_to(target, (PREFIX, CACHE))
         pick = jnp.where(match, 1.0, 0.0).astype(jnp.bfloat16)
         chosen.append(jnp.dot(pick, pbuf[kv], preferred_element_type=jnp.float32).astype(jnp.bfloat16))
+
+    w_complete()
+    for i in range(3):
+        columns = slice(i * COLS, (i + 1) * COLS)
+        far = product(i, [(hh, lax.rem(places[hh][0] + 2, 4)) for hh in range(2)])
+        qkv[:, columns] = (acc[:, columns] + far).astype(jnp.bfloat16)
 
     low = lax.broadcasted_iota(jnp.int32, (128, 128), 1) < 64
     keys, values = [], []
@@ -516,7 +519,8 @@
 
     send_table.wait_send()
     for hh in range(2):
-        weight_piece(hh).wait_send()
+        for part in range(2):
+            weight_piece(hh, part).wait_send()
         for d in range(1, 4):
             out_piece(d, hh).wait_send()
         for k in range(2):
@@ -625,7 +629,7 @@
             pltpu.VMEM((TP, ROWS, COLS), bf16),
             pltpu.VMEM((TP, ROWS, COLS), bf16),
             dma((7,)), dma((CH,)), dma((4, CH)), dma((4, CH)), dma((4, CH)),
-            dma((2,)), dma((2,)), dma((1,)), dma((1,)), dma((4, 2)), dma((4, 2)), dma((3, 2)), dma((3, 2)),
+            dma((2, 2)), dma((2, 2)), dma((1,)), dma((1,)), dma((4, 2)), dma((4, 2)), dma((3, 2)), dma((3, 2)),
             dma((2, 2, 6)), dma((2, 2, 6)), dma((2, 2, 6)), dma((2, 2, 6)), dma((2, 2, 6)), dma((2, 2, 6)),
             dma((2, 2, 2)), dma((2, 2, 2, 2)), dma((2, 2, 2)), dma((2, 2, 2)), dma((2,)), dma((2,)),
             dma((2, 4)), dma((2, 4)), dma((4,)), dma((4,)),

time: 70.7 us -> 67.4 us (0.953)
  Pallas kernels: 68.6 us -> 65.3 us
    pallas_call x1, Pallas kernels: 68.6 us -> 65.3 us  [body(): pl.pallas_call(kernel, name='sublayer', out_shape=jax.ShapeDtypeStruct((R...]
where the time goes in v5:
time: 67.4 us; the launch traced here: 67.2 us
  Pallas kernels  65.3 us (97%)
  local copies, waits for them, and re-layouts  1.88 us (3%)
    pallas_call x1, Pallas kernels, body(): pl.pallas_call(kernel, name='sublayer', out_shape=jax.ShapeDtypeStruct((R...  65.3 us
    unnamed x1, local copies, waits for them, and re-layouts  1.88 us

profile of v5, /device:TPU:1, one launch (start us, length us, event | category | flops | bytes accessed | tf_op | source)
XLA Modules:
  0.0 67.2 jit_solution(12379933338285630852)
XLA Ops:
  0.0 65.3 %sublayer.1 = bf16[128,2048]{1,0:T(8,128)(2,1)} custom-call(s32[64]{0:T(128)} %request_ref.1, s32[64]{0:T(128)} %block_ref.1, s32[64]{0:T(128)} %length_ref.1, bf16[128,2048]{1,0:T(8,128)(2,1)} %bitcast.8, bf16[16,128]{1,0:T(8,128)(2,1)} %bitcast.9, bf16[3,2048,512]{2,1,0:T(8,128)(2,1)} %bitcast.6, bf16[8,2,512]{2,1,0:T(2,128)(2,1)} %pref.1, ...), custom_call_target="tpu_custom_call" | custom-call | tf_op jit(solution)/shard_map/sublayer/pallas_call | solution.py:609
  65.4 1.9 %copy.12 = bf16[1,128,2048]{2,1,0:T(8,128)(2,1)} copy(bf16[1,128,2048]{2,1,0:T(8,128)(2,1)} %bitcast.7) | data formatting | bytes 1048576

commit v6 on v5

--- a/solution.py
+++ b/solution.py
@@ -463,7 +463,9 @@
         )
 
     def attend(r):
-        for p in range(HEADS // 2):
+        pairs = range(HEADS // 2)
+        scores = []
+        for p in pairs:
             lanes = slice(p * 128, p * 128 + 128)
             query = qkv[r * 128 : r * 128 + 128, lanes]
             zero = jnp.zeros_like(query)
@@ -473,13 +475,18 @@
                 key = keys[p] if kb == 0 else qkv[kb * 128 - 128 : kb * 128, COLS + p * 128 : COLS + p * 128 + 128]
                 part = lax.dot_general(key, stacked, (((1,), (1,)), ((), ())), preferred_element_type=jnp.float32)
                 blocks.append(part + tiles[p, r + 1 - kb])
+            scores.append(blocks)
+        weighed = []
+        for blocks in scores:
             top = functools.reduce(jnp.maximum, [jnp.max(b, 0, keepdims=True) for b in blocks])
             probs = [jnp.exp(b - top) for b in blocks]
             denom = functools.reduce(jnp.add, [jnp.sum(b, 0, keepdims=True) for b in probs])
-            probs = jnp.concatenate([b.astype(jnp.bfloat16) for b in probs], 0)
-            out = jnp.dot(values[p][:, : (r + 2) * 128], probs, preferred_element_type=jnp.float32) / denom
+            weighed.append((jnp.concatenate([b.astype(jnp.bfloat16) for b in probs], 0), denom))
+        for p in pairs:
+            probs, denom = weighed[p]
+            out = jnp.dot(values[p][:, : (r + 2) * 128], probs, preferred_element_type=jnp.float32) * (1.0 / denom)
             pair = jnp.concatenate([out[:64, :128], out[64:, 128:]], 0)
-            asend[r, :, lanes] = pair.T.astype(jnp.bfloat16)
+            asend[r, :, p * 128 : p * 128 + 128] = pair.T.astype(jnp.bfloat16)
 
     def attn_copy(r):
         return remote(asend.at[r], aall.at[group], at_s.at[r], at_r.at[group], at(zh, side, r))

time: 67.4 us -> 66.8 us (level)
  no operation moved by 1% of the time
where the time goes in v6:
time: 66.8 us; the launch traced here: 66.6 us
  Pallas kernels  64.7 us (97%)
  local copies, waits for them, and re-layouts  1.88 us (3%)
    pallas_call x1, Pallas kernels, body(): pl.pallas_call(kernel, name='sublayer', out_shape=jax.ShapeDtypeStruct((R...  64.7 us
    unnamed x1, local copies, waits for them, and re-layouts  1.88 us

profile of v6, /device:TPU:1, one launch (start us, length us, event | category | flops | bytes accessed | tf_op | source)
XLA Modules:
  0.0 66.6 jit_solution(10460161623607016013)
XLA Ops:
  0.0 64.7 %sublayer.1 = bf16[128,2048]{1,0:T(8,128)(2,1)} custom-call(s32[64]{0:T(128)} %request_ref.1, s32[64]{0:T(128)} %block_ref.1, s32[64]{0:T(128)} %length_ref.1, bf16[128,2048]{1,0:T(8,128)(2,1)} %bitcast.8, bf16[16,128]{1,0:T(8,128)(2,1)} %bitcast.9, bf16[3,2048,512]{2,1,0:T(8,128)(2,1)} %bitcast.6, bf16[8,2,512]{2,1,0:T(2,128)(2,1)} %pref.1, ...), custom_call_target="tpu_custom_call" | custom-call | tf_op jit(solution)/shard_map/sublayer/pallas_call | solution.py:616
  64.8 1.9 %copy.12 = bf16[1,128,2048]{2,1,0:T(8,128)(2,1)} copy(bf16[1,128,2048]{2,1,0:T(8,128)(2,1)} %bitcast.7) | data formatting | bytes 1048576
